TPU v7x, 512 devices: a whole 4x8x8 slice. The times are simulated.
512 devices in a mesh: recv: 32 (over x, z_lo, core), src: 16 (over y, z_hi).
Axes of the slice: x: 4, y: 8, z: 8 (z_hi: 2, z_lo: 4; z = z_hi * 4 + z_lo), core: 2. Of those that a mesh axis runs over, the one named last changes fastest.
Arguments:
- record: bfloat16 [512, 131072], P('recv', 'src'), may hold values from -41 to 41
- source_channel: int32 [32], replicated, may hold values from 0 to 511, as said below
- band_edges: int32 [32, 2], replicated, may hold values from 0 to 512, as said below
- offsets: int32 [16], replicated, may hold values from 0 to 5376, as said below
Outputs:
- virtual_gathers: float32 [32, 512, 256], P('src', 'recv')
Inputs may be any that keep to these rules, and one draw needn't show every extreme that they name: `source_channel`: the 32 channels are distinct. band_edges[s, 0] < band_edges[s, 1] for every source. `offsets`: window w lies inside time shard w.
All inputs are finite; a program needn't handle non-finite values.
Results may differ from a plain program's by a relative error of at most 0.0041.
Values may be sent and summed in bfloat16 or wider, within the bound.
No kernel may reach another device: no remote copies, remote signals or barrier semaphores. Data moves between devices by JAX's collectives and lax.ppermute only.
A program may use at most 64 MiB of HBM per device.

v0:
```python
import jax
import jax.numpy as jnp
from jax import lax
from jax.sharding import PartitionSpec as P

WL = 2560
L = 256


EPSILON = 1e-06


def whiten(segment):
    values = segment.astype(jnp.float32)
    spread = jnp.sqrt(jnp.mean(values * values, axis=-1, keepdims=True) + EPSILON)
    return (values / spread).astype(jnp.bfloat16)


def correlate_group(group_rows, recv_rows):
    seg_len = recv_rows.shape[1]
    row_count = group_rows.shape[0]
    source_part = group_rows[:, L // 2 : L // 2 + WL]
    zero_tail = jnp.zeros((row_count, seg_len + 1 - WL), jnp.bfloat16)
    padded = jnp.concatenate([source_part, zero_tail], axis=1)
    tiled = jnp.tile(padded, (1, L))[:, : L * seg_len].reshape(row_count, L, seg_len)
    return jnp.einsum("skt,rt->srk", tiled, recv_rows, preferred_element_type=jnp.float32)


def correlate(source_rows, recv_rows):
    row_count = source_rows.shape[0]
    group_size = 2
    grouped = source_rows.reshape(row_count // group_size, group_size, source_rows.shape[1])
    results = lax.map(lambda group_rows: correlate_group(group_rows, recv_rows), grouped)
    return results.reshape(row_count, recv_rows.shape[0], L)


def local(record, source_channel, band_edges, offsets):
    chan_dev = record.shape[0]
    seg_len = WL + L
    recv_index = lax.axis_index("recv")
    src_index = lax.axis_index("src")
    src_count = lax.axis_size("src")
    source_total = source_channel.shape[0]
    source_block = source_total // src_count
    window_start = lax.dynamic_index_in_dim(offsets, src_index, 0, keepdims=False)
    segment = lax.dynamic_slice(record, (jnp.int32(0), window_start), (chan_dev, seg_len))
    recv_rows = whiten(segment)
    channel_ids = recv_index * chan_dev + jnp.arange(chan_dev, dtype=jnp.int32)
    selector = (source_channel[:, None] == channel_ids[None, :]).astype(jnp.bfloat16)
    picked = jnp.dot(selector, segment, preferred_element_type=jnp.float32)
    source_raw = lax.psum(picked.astype(jnp.bfloat16), "recv")
    source_rows = whiten(source_raw)
    own_sources = lax.all_to_all(
        source_rows[:, None, :], "src", split_axis=0, concat_axis=1, tiled=True
    )
    initial = jnp.zeros((source_block, chan_dev, L), jnp.float32)
    shard_piece = lax.all_gather(recv_rows[None], "src", axis=0, tiled=True)

    def one_window(number, carried):
        recv_piece = lax.dynamic_index_in_dim(shard_piece, number, 0, keepdims=False)
        source_piece = lax.dynamic_index_in_dim(own_sources, number, 1, keepdims=False)
        return carried + correlate(source_piece, recv_piece)

    stacked = lax.fori_loop(0, shard_piece.shape[0], one_window, initial)
    factor = 1.0 / float(WL * src_count) ** 0.5
    own_channel = lax.dynamic_slice_in_dim(
        source_channel, src_index * source_block, source_block, 0
    )
    own_edges = lax.dynamic_slice_in_dim(band_edges, src_index * source_block, source_block, 0)
    in_band = (channel_ids[None, :] >= own_edges[:, 0:1]) & (
        channel_ids[None, :] < own_edges[:, 1:2]
    )
    in_band = in_band & (channel_ids[None, :] != own_channel[:, None])
    return jnp.where(in_band[:, :, None], stacked * factor, jnp.float32(0.0))


def solution(mesh):
    in_specs = (P("recv", "src"), P(), P(), P())
    out_specs = P("src", "recv", None)
    return jax.shard_map(local, mesh=mesh, in_specs=in_specs, out_specs=out_specs, check_vma=False)
```

profile of v0, /device:TPU:1, one launch (start us, length us, event | category | flops | bytes accessed | tf_op | source)
XLA Modules:
  0.0 636.6 jit_solution(3919369733604993040)
XLA Ops:
  16.1 280.7 %all-reduce.3.cloned.1.call-done = bf16[32,2816]{1,0:T(8,128)(2,1)} async-done(((bf16[32,2816]{1,0:T(8,128)(2,1)}), bf16[32,2816]{1,0:T(8,128)(2,1)}) %all-reduce.3.cloned.1.call-update) | async-done | bytes 180240 | tf_op jit(solution)/shard_map/psum | solution.py:51
  300.8 10.0 %all-to-all-start = ((bf16[16,2,2816]{2,1,0:T(2,128)(2,1)}), bf16[16,2,2816]{2,1,0:T(2,128)(2,1)S(1)}, u32[]{:S(2)}, u32[]{:S(2)}) async-start(bf16[16,2,2816]{2,1,0:T(2,128)(2,1)} %reshape.136), calls=%async_computation | async-start | bytes 360448 | tf_op jit(solution)/shard_map/all_to_all | solution.py:53
  310.8 12.7 %all-to-all-done = bf16[16,2,2816]{2,1,0:T(2,128)(2,1)S(1)} async-done(((bf16[16,2,2816]{2,1,0:T(2,128)(2,1)}), bf16[16,2,2816]{2,1,0:T(2,128)(2,1)S(1)}, u32[]{:S(2)}, u32[]{:S(2)}) %all-to-all-start) | async-done | bytes 180256 | tf_op jit(solution)/shard_map/all_to_all | solution.py:53
  324.9 303.5 %while.22 = (s32[]{:T(128)}, f32[2,16,256]{2,1,0:T(8,128)S(1)}, bf16[16,16,2816]{2,1,0:T(8,128)(2,1)}, bf16[2,16,2816]{2,0,1:T(2,128)(2,1)S(1)}, s32[]{:T(128)}, /*index=5*/bf16[]{:T(256)}, s32[]{:T(128)}) while((s32[]{:T(128)}, f32[2,16,256]{2,1,0:T(8,128)S(1)}, bf16[16,16,2816]{2,1,0:T(8,128)(2,1)}, ...), condition=%wide.region_4.5_spmd.clone, body=%wide.region_3.4_spmd.clone.sunk | while | flops 46153728 | bytes 23305828 | solution.py:64
  325.2 6.4 %reshape.139 = bf16[1442304]{0:T(1024)(128)(2,1)} reshape(bf16[2,256,2817]{2,1,0:T(8,128)(2,1)S(1)} %tile.30) | data formatting | bytes 5769216 | tf_op jit(solution)/shard_map/while
  331.6 5.8 tile.31
  337.4 3.7 slice.39
  344.1 6.4 %reshape.139 = bf16[1442304]{0:T(1024)(128)(2,1)} reshape(bf16[2,256,2817]{2,1,0:T(8,128)(2,1)S(1)} %tile.30) | data formatting | bytes 5769216 | tf_op jit(solution)/shard_map/while
  350.6 5.8 tile.31
  356.4 3.7 slice.39
  363.1 6.4 %reshape.139 = bf16[1442304]{0:T(1024)(128)(2,1)} reshape(bf16[2,256,2817]{2,1,0:T(8,128)(2,1)S(1)} %tile.30) | data formatting | bytes 5769216 | tf_op jit(solution)/shard_map/while
  369.5 5.8 tile.31
  375.4 3.7 slice.39
  382.1 6.4 %reshape.139 = bf16[1442304]{0:T(1024)(128)(2,1)} reshape(bf16[2,256,2817]{2,1,0:T(8,128)(2,1)S(1)} %tile.30) | data formatting | bytes 5769216 | tf_op jit(solution)/shard_map/while
  388.5 5.8 tile.31
  394.3 3.7 slice.39
  401.1 6.4 %reshape.139 = bf16[1442304]{0:T(1024)(128)(2,1)} reshape(bf16[2,256,2817]{2,1,0:T(8,128)(2,1)S(1)} %tile.30) | data formatting | bytes 5769216 | tf_op jit(solution)/shard_map/while
  407.5 5.8 tile.31
  413.3 3.7 slice.39
  420.0 6.4 %reshape.139 = bf16[1442304]{0:T(1024)(128)(2,1)} reshape(bf16[2,256,2817]{2,1,0:T(8,128)(2,1)S(1)} %tile.30) | data formatting | bytes 5769216 | tf_op jit(solution)/shard_map/while
  426.4 5.8 tile.31
  432.3 3.7 slice.39
  439.0 6.4 %reshape.139 = bf16[1442304]{0:T(1024)(128)(2,1)} reshape(bf16[2,256,2817]{2,1,0:T(8,128)(2,1)S(1)} %tile.30) | data formatting | bytes 5769216 | tf_op jit(solution)/shard_map/while
  445.4 5.8 tile.31
  451.2 3.7 slice.39
  458.0 6.4 %reshape.139 = bf16[1442304]{0:T(1024)(128)(2,1)} reshape(bf16[2,256,2817]{2,1,0:T(8,128)(2,1)S(1)} %tile.30) | data formatting | bytes 5769216 | tf_op jit(solution)/shard_map/while
  464.4 5.8 tile.31
  470.2 3.7 slice.39
  476.9 6.4 %reshape.139 = bf16[1442304]{0:T(1024)(128)(2,1)} reshape(bf16[2,256,2817]{2,1,0:T(8,128)(2,1)S(1)} %tile.30) | data formatting | bytes 5769216 | tf_op jit(solution)/shard_map/while
  483.4 5.8 tile.31
  489.2 3.7 slice.39
  495.9 6.4 %reshape.139 = bf16[1442304]{0:T(1024)(128)(2,1)} reshape(bf16[2,256,2817]{2,1,0:T(8,128)(2,1)S(1)} %tile.30) | data formatting | bytes 5769216 | tf_op jit(solution)/shard_map/while
  502.3 5.8 tile.31
  508.1 3.7 slice.39
  514.9 6.4 %reshape.139 = bf16[1442304]{0:T(1024)(128)(2,1)} reshape(bf16[2,256,2817]{2,1,0:T(8,128)(2,1)S(1)} %tile.30) | data formatting | bytes 5769216 | tf_op jit(solution)/shard_map/while
  521.3 5.8 tile.31
  527.1 3.7 slice.39
  533.8 6.4 %reshape.139 = bf16[1442304]{0:T(1024)(128)(2,1)} reshape(bf16[2,256,2817]{2,1,0:T(8,128)(2,1)S(1)} %tile.30) | data formatting | bytes 5769216 | tf_op jit(solution)/shard_map/while
  540.3 5.8 tile.31
  546.1 3.7 slice.39
  552.8 6.4 %reshape.139 = bf16[1442304]{0:T(1024)(128)(2,1)} reshape(bf16[2,256,2817]{2,1,0:T(8,128)(2,1)S(1)} %tile.30) | data formatting | bytes 5769216 | tf_op jit(solution)/shard_map/while
  559.2 5.8 tile.31
  571.8 6.4 %reshape.139 = bf16[1442304]{0:T(1024)(128)(2,1)} reshape(bf16[2,256,2817]{2,1,0:T(8,128)(2,1)S(1)} %tile.30) | data formatting | bytes 5769216 | tf_op jit(solution)/shard_map/while
  578.2 5.8 tile.31
  590.8 6.4 %reshape.139 = bf16[1442304]{0:T(1024)(128)(2,1)} reshape(bf16[2,256,2817]{2,1,0:T(8,128)(2,1)S(1)} %tile.30) | data formatting | bytes 5769216 | tf_op jit(solution)/shard_map/while
  597.2 5.8 tile.31
  609.7 6.4 %reshape.139 = bf16[1442304]{0:T(1024)(128)(2,1)} reshape(bf16[2,256,2817]{2,1,0:T(8,128)(2,1)S(1)} %tile.30) | data formatting | bytes 5769216 | tf_op jit(solution)/shard_map/while
  616.1 5.8 tile.31
  (112 shorter events, 75.2 us)
Async XLA Ops:
  7.4 8.7 %copy-start = (s32[32,2]{0,1:T(2,128)S(1)}, s32[32,2]{0,1:T(2,128)}, u32[]{:S(2)}) copy-start(s32[32,2]{0,1:T(2,128)} %param.8) | copy-start | bytes 772
  7.4 289.4 %all-reduce.3.cloned.1.call-start = ((), (), s32[]{:S(2)}) async-start(), calls=%async_computation.1 | async-start | bytes 360448 | tf_op jit(solution)/shard_map/psum | solution.py:51
  12.5 312.4 %all-gather.3.cloned.1.call-start = ((), (), s32[]{:S(2)}) async-start(), calls=%async_computation.2 | async-start | bytes 1531904 | tf_op jit(solution)/shard_map/all_gather | solution.py:57
  300.8 22.8 %all-to-all-start = ((bf16[16,2,2816]{2,1,0:T(2,128)(2,1)}), bf16[16,2,2816]{2,1,0:T(2,128)(2,1)S(1)}, u32[]{:S(2)}, u32[]{:S(2)}) async-start(bf16[16,2,2816]{2,1,0:T(2,128)(2,1)} %reshape.136), calls=%async_computation | async-start | bytes 360448 | tf_op jit(solution)/shard_map/all_to_all | solution.py:53
Sparse Core Ops, SparseCore 0:
  12.6 284.1 all-reduce.2
Sparse Core Ops, SparseCore 1:
  16.1 100.0 all-gather.2
where the time goes:
time: 641 us; the launch traced here: 637 us
  waiting for transfers between devices  293 us (46%)
  local copies, waits for them, and re-layouts  263 us (41%)
  matrix products  45.2 us (7%)
  between operations  16.9 us (3%)
  starting transfers between devices  10 us (2%)
  other arithmetic  7.37 us (1%)
    psum x1, waiting for transfers between devices, local(): source_raw = lax.psum(picked.astype(jnp.bfloat16), 'recv')  281 us
    while x16, local copies, waits for them, and re-layouts  103 us
    another operation x32, local copies, waits for them, and re-layouts, correlate_group(): jnp.tile(padded, (1, L))[:, :L * seg_len].reshape(row_count, L, seg_len)  96.1 us
    slice x16, local copies, waits for them, and re-layouts, correlate_group(): jnp.tile(padded, (1, L))[:, :L * seg_len].reshape(row_count, L, seg_len)  59.8 us
    dot_general x16, matrix products, correlate_group(): jnp.einsum('skt,rt->srk', tiled, recv_rows, preferred_element_type=jnp.fl...  43.4 us
  transfers between devices with their start and end apart: 3, of which 2 were waited for; matrix products, arithmetic and copies ran while one was open for 1% of the time, Pallas kernels for 0%

commit v1 on v0

v1 whole, which is shorter than its diff:
```python
import jax
import jax.numpy as jnp
from jax import lax
from jax.experimental import pallas as pl
from jax.experimental.pallas import tpu as pltpu
from jax.sharding import PartitionSpec as P

WL = 2560
L = 256
SEG = WL + L
LANES = 128
TILES = SEG // LANES
BODY = WL // LANES
SLOT = 24
STEP = 16
EPSILON = 1e-06

VMEM = pl.BlockSpec(memory_space=pltpu.VMEM)
SMEM = pl.BlockSpec(memory_space=pltpu.SMEM)


def lane_index(rows):
    return lax.broadcasted_iota(jnp.int32, (rows, LANES), 1)


def prepare_kernel(where_ref, row_ref, record_ref, white_ref, slots_ref, line_ref):
    chan_dev = record_ref.shape[0]
    start = where_ref[0]
    first = start // LANES
    rest = start - first * LANES
    last = record_ref.shape[1] // LANES - 1
    lane = lane_index(chan_dev)
    shift = lax.rem(LANES - rest, LANES)

    def rolled(tile):
        at = pl.multiple_of(jnp.minimum(first + tile, last) * LANES, LANES)
        return pltpu.roll(record_ref[:, pl.ds(at, LANES)].astype(jnp.float32), shift, 1)

    segment = []
    total = jnp.zeros((chan_dev, LANES), jnp.float32)
    left = rolled(0)
    for tile in range(TILES):
        right = rolled(tile + 1)
        piece = jnp.where(lane < LANES - rest, left, right)
        segment.append(piece)
        total = total + piece * piece
        left = right
    power = jnp.sum(total, axis=1, keepdims=True) / SEG
    spread = jnp.broadcast_to(jnp.sqrt(power + EPSILON), (chan_dev, LANES))
    line_ref[...] = jnp.zeros_like(line_ref)
    for tile in range(TILES):
        white = (segment[tile] / spread).astype(jnp.bfloat16)
        white_ref[:, tile * LANES : (tile + 1) * LANES] = white
        if 1 <= tile <= BODY:
            line_ref[pl.ds(tile - 1, chan_dev, stride=SLOT), :] = white.astype(jnp.float32)
    for slot in range(slots_ref.shape[0]):
        at = pl.multiple_of(row_ref[slot] * SLOT, 8)
        slots_ref[slot] = line_ref[pl.ds(at, SLOT), :].astype(jnp.bfloat16)


def spread_kernel(owner_ref, slots_ref, out_ref):
    row = slots_ref[owner_ref[0]]
    for slot in range(out_ref.shape[0]):
        out_ref[slot] = row


def correlate_kernel(source_ref, white_ref, out_ref, line_ref, a_ref, b_ref, part_ref):
    count = source_ref.shape[0]
    chan_dev = white_ref.shape[0]
    lane = lane_index(count)
    for slot in range(count):
        line_ref[slot * SLOT : (slot + 1) * SLOT, :] = source_ref[slot].astype(jnp.float32)
    coarse = LANES // STEP
    pieces = [line_ref[pl.ds(tile, count, stride=SLOT), :] for tile in range(BODY)]
    zero = jnp.zeros((count, LANES), jnp.float32)
    for m in range(coarse):
        shift = STEP * m
        left = zero
        for tile in range(BODY + 1):
            right = pieces[tile] if tile < BODY else zero
            if m:
                right = pltpu.roll(right, shift, 1) if tile < BODY else zero
                value = jnp.where(lane < shift, left, right)
            else:
                value = right
            a_ref[m * count : (m + 1) * count, tile * LANES : (tile + 1) * LANES] = value.astype(jnp.bfloat16)
            left = right
    lane = lane_index(chan_dev)
    pieces = [white_ref[:, tile * LANES : (tile + 1) * LANES].astype(jnp.float32) for tile in range(TILES)]
    for l in range(STEP):
        left = pltpu.roll(pieces[0], LANES - l, 1) if l else pieces[0]
        for tile in range(TILES):
            right = pieces[(tile + 1) % TILES]
            if l:
                right = pltpu.roll(right, LANES - l, 1)
                value = jnp.where(lane < LANES - l, left, right)
            else:
                value = left
            b_ref[l * chan_dev : (l + 1) * chan_dev, tile * LANES : (tile + 1) * LANES] = value.astype(jnp.bfloat16)
            left = right
    depth = (BODY + 1) * LANES
    half = count // 2
    for high in range(L // LANES):
        product = lax.dot_general(
            a_ref[...],
            b_ref[:, high * LANES : high * LANES + depth],
            (((1,), (1,)), ((), ())),
            preferred_element_type=jnp.float32,
        )
        for low in range(coarse):
            m = high * coarse + low
            for j in range(2):
                row = low * count + j * half
                for n in range(STEP * chan_dev // LANES):
                    part_ref[n, pl.ds(j * STEP + m, half, stride=2 * STEP), :] = product[
                        row : row + half, n * LANES : (n + 1) * LANES
                    ]
    for n in range(STEP * chan_dev // LANES):
        out_ref[:, n * LANES : (n + 1) * LANES] = part_ref[n].astype(jnp.bfloat16)


def local(record, source_channel, band_edges, offsets):
    chan_dev = record.shape[0]
    recv_index = lax.axis_index("recv")
    src_index = lax.axis_index("src")
    src_count = lax.axis_size("src")
    source_total = source_channel.shape[0]
    per = source_total // src_count
    slot_channel = source_channel.reshape(src_count, per).T.reshape(source_total)
    window_start = lax.dynamic_slice(offsets, (src_index,), (1,))
    rows = jnp.clip(slot_channel - recv_index * chan_dev, 0, chan_dev - 1)
    owner = lax.dynamic_slice(slot_channel, (recv_index,), (1,)) // chan_dev
    params = pltpu.CompilerParams(vmem_limit_bytes=40 * 1024 * 1024)
    slots = jax.ShapeDtypeStruct((source_total, SLOT, LANES), jnp.bfloat16)
    white, out_rows = pl.pallas_call(
        prepare_kernel,
        out_shape=(jax.ShapeDtypeStruct((chan_dev, SEG), jnp.bfloat16), slots),
        in_specs=[SMEM, SMEM, VMEM],
        out_specs=(VMEM, VMEM),
        scratch_shapes=[pltpu.VMEM((chan_dev * SLOT, LANES), jnp.float32)],
        compiler_params=params,
        name="prepare",
    )(window_start, rows, record)
    in_rows = lax.all_to_all(out_rows, "recv", split_axis=0, concat_axis=0, tiled=True)
    own_row = pl.pallas_call(
        spread_kernel,
        out_shape=slots,
        in_specs=[SMEM, VMEM],
        out_specs=VMEM,
        compiler_params=params,
        name="spread",
    )(owner, in_rows)
    sources = lax.all_to_all(own_row, "recv", split_axis=0, concat_axis=0, tiled=True)
    wide = STEP * chan_dev
    partial = pl.pallas_call(
        correlate_kernel,
        out_shape=jax.ShapeDtypeStruct((source_total * (L // STEP), wide), jnp.bfloat16),
        in_specs=[VMEM, VMEM],
        out_specs=VMEM,
        scratch_shapes=[
            pltpu.VMEM((source_total * SLOT, LANES), jnp.float32),
            pltpu.VMEM((source_total * LANES // STEP, (BODY + 1) * LANES), jnp.bfloat16),
            pltpu.VMEM((wide, SEG), jnp.bfloat16),
            pltpu.VMEM((wide // LANES, source_total * (L // STEP), LANES), jnp.float32),
        ],
        compiler_params=params,
        name="correlate",
    )(sources, white)
    partial = partial.reshape(src_count, per * (L // STEP), wide)
    windows = lax.all_to_all(partial, "src", split_axis=0, concat_axis=0, tiled=True)
    stacked = jnp.sum(windows.astype(jnp.float32), axis=0)
    stacked = stacked.reshape(per, L // STEP, STEP, chan_dev).transpose(0, 3, 1, 2).reshape(per, chan_dev, L)
    factor = 1.0 / float(WL * src_count) ** 0.5
    own_channel = lax.dynamic_slice_in_dim(source_channel, src_index * per, per, 0)
    own_edges = lax.dynamic_slice_in_dim(band_edges, src_index * per, per, 0)
    channel_ids = recv_index * chan_dev + jnp.arange(chan_dev, dtype=jnp.int32)
    in_band = (channel_ids[None, :] >= own_edges[:, 0:1]) & (channel_ids[None, :] < own_edges[:, 1:2])
    in_band = in_band & (channel_ids[None, :] != own_channel[:, None])
    return jnp.where(in_band[:, :, None], stacked * factor, jnp.float32(0.0))


def solution(mesh):
    in_specs = (P("recv", "src"), P(), P(), P())
    out_specs = P("src", "recv", None)
    return jax.shard_map(local, mesh=mesh, in_specs=in_specs, out_specs=out_specs, check_vma=False)
```

time: 641 us -> 72.6 us (0.11)
  waiting for transfers between devices: 293 us -> 31.7 us
  local copies, waits for them, and re-layouts: 263 us -> 4.08 us
  matrix products: 45.2 us -> 0 us
  starting transfers between devices: 10 us -> 27.7 us
  between operations: 16.9 us -> 2.68 us
  other arithmetic: 7.37 us -> 0.83 us
    psum x1 -> x0, waiting for transfers between devices: 281 us -> none  [local(): source_raw = lax.psum(picked.astype(jnp.bfloat16), 'recv')]
    while x16 -> x0, local copies, waits for them, and re-layouts: 103 us -> none
    another operation x32 -> x0, local copies, waits for them, and re-layouts: 96.1 us -> none  [correlate_group(): jnp.tile(padded, (1, L))[:, :L * seg_len].reshape(row_count, L, seg_len)]
    slice x32 -> x0, local copies, waits for them, and re-layouts: 60 us -> none  [the longest x16 59.8 us: correlate_group(): jnp.tile(padded, (1, L))[:, :L * seg_len].reshape(row_count, L, seg_len)]
    dot_general x17 -> x0, matrix products: 45.2 us -> none  [the longest x16 43.4 us: correlate_group(): jnp.einsum('skt,rt->srk', tiled, recv_rows, preferred_element_type=jnp.fl...]
    all_to_all x1 -> x3, waiting for transfers between devices: 12.7 us -> 31.7 us  [the longest x1 15.1 us: local(): lax.all_to_all(partial, 'src', split_axis=0, concat_axis=0, tiled=True)]
    all_to_all x1 -> x3, starting transfers between devices: 9.97 us -> 27.7 us  [the longest x1 12.7 us: local(): lax.all_to_all(partial, 'src', split_axis=0, concat_axis=0, tiled=True)]
  transfers between devices with their start and end apart: 3 -> 3, of which waited for: 2 -> 3; matrix products, arithmetic and copies ran while one was open for 1% -> 1% of each run, Pallas kernels for 0% -> 0%
where the time goes in v1:
time: 72.6 us; the launch traced here: 72.2 us
  waiting for transfers between devices  31.7 us (44%)
  starting transfers between devices  27.7 us (38%)
  Pallas kernels  5.21 us (7%)
  local copies, waits for them, and re-layouts  4.08 us (6%)
  between operations  2.68 us (4%)
  other arithmetic  0.83 us (1%)
    all_to_all x1, waiting for transfers between devices, local(): lax.all_to_all(partial, 'src', split_axis=0, concat_axis=0, tiled=True)  15.1 us
    all_to_all x1, starting transfers between devices, local(): lax.all_to_all(partial, 'src', split_axis=0, concat_axis=0, tiled=True)  12.7 us
    all_to_all x1, starting transfers between devices, local(): lax.all_to_all(out_rows, 'recv', split_axis=0, concat_axis=0, tiled=True)  11.4 us
    all_to_all x1, waiting for transfers between devices, local(): lax.all_to_all(own_row, 'recv', split_axis=0, concat_axis=0, tiled=True)  9.82 us
    all_to_all x1, waiting for transfers between devices, local(): lax.all_to_all(out_rows, 'recv', split_axis=0, concat_axis=0, tiled=True)  6.7 us
    all_to_all x1, starting transfers between devices, local(): lax.all_to_all(own_row, 'recv', split_axis=0, concat_axis=0, tiled=True)  3.65 us
    pallas_call x1, Pallas kernels, local(): pl.pallas_call(correlate_kernel, out_shape=jax.ShapeDtypeStruct((source_t...  2.37 us
    unnamed x8, local copies, waits for them, and re-layouts  2.29 us
  transfers between devices with their start and end apart: 3, of which 3 were waited for; matrix products, arithmetic and copies ran while one was open for 1% of the time, Pallas kernels for 0%

profile of v1, /device:TPU:1, one launch (start us, length us, event | category | flops | bytes accessed | tf_op | source)
XLA Modules:
  0.0 72.2 jit_solution(11018947019893158719)
XLA Ops:
  0.0 0.0 copy-start
  0.0 0.0 copy-start.2
  0.0 0.7 copy-done.2
  0.7 0.1 reshape.111
  0.8 0.1 copy.6
  0.8 0.1 reshape.112
  0.9 0.0 copy-start.3
  0.9 0.7 copy-done.3
  1.6 0.6 dynamic_slice.15.where_ref
  2.2 0.0 copy-start.1
  2.2 0.9 %copy-done.1 = bf16[16,8192]{1,0:T(8,128)(2,1)S(1)} copy-done((bf16[16,8192]{1,0:T(8,128)(2,1)S(1)}, bf16[16,8192]{1,0:T(8,128)(2,1)}, u32[]{:S(2)}) %copy-start.1) | copy-done | bytes 262168
  3.1 2.1 %prepare.1 = (bf16[16,2816]{1,0:T(8,128)(2,1)S(1)}, bf16[32,24,128]{2,1,0:T(8,128)(2,1)}) custom-call(s32[1]{0:T(128)} %dynamic_slice.15.where_ref, s32[32]{0:T(128)S(1)} %subtract_clamp_fusion.row_ref, bf16[16,8192]{1,0:T(8,128)(2,1)S(1)} %copy-done.1), custom_call_target="tpu_custom_call" | custom-call | tf_op jit(solution)/shard_map/prepare/pallas_call | solution.py:135
  5.3 11.4 %all-to-all-start = ((bf16[32,24,128]{2,1,0:T(8,128)(2,1)}), bf16[32,24,128]{2,1,0:T(8,128)(2,1)S(1)}, u32[]{:S(2)}, u32[]{:S(2)}) async-start(bf16[32,24,128]{2,1,0:T(8,128)(2,1)} %get-tuple-element.7), calls=%async_computation | async-start | bytes 393216 | tf_op jit(solution)/shard_map/all_to_all | solution.py:144
  16.7 0.6 dynamic_slice.14
  19.8 6.7 %all-to-all-done.slots_ref = bf16[32,24,128]{2,1,0:T(8,128)(2,1)S(1)} async-done(((bf16[32,24,128]{2,1,0:T(8,128)(2,1)}), bf16[32,24,128]{2,1,0:T(8,128)(2,1)S(1)}, u32[]{:S(2)}, u32[]{:S(2)}) %all-to-all-start) | async-done | bytes 196640 | tf_op jit(solution)/shard_map/all_to_all | solution.py:144
  26.6 0.7 spread.1
  27.2 3.6 %all-to-all-start.1 = ((bf16[32,24,128]{2,1,0:T(8,128)(2,1)}), bf16[32,24,128]{2,1,0:T(8,128)(2,1)S(1)}, u32[]{:S(2)}, u32[]{:S(2)}) async-start(bf16[32,24,128]{2,1,0:T(8,128)(2,1)} %spread.1), calls=%async_computation.1 | async-start | bytes 393216 | tf_op jit(solution)/shard_map/all_to_all | solution.py:153
  30.9 0.0 copy-done
  30.9 0.1 constant_dynamic-slice_fusion
  31.0 9.8 %all-to-all-done.1.source_ref = bf16[32,24,128]{2,1,0:T(8,128)(2,1)S(1)} async-done(((bf16[32,24,128]{2,1,0:T(8,128)(2,1)}), bf16[32,24,128]{2,1,0:T(8,128)(2,1)S(1)}, u32[]{:S(2)}, u32[]{:S(2)}) %all-to-all-start.1) | async-done | bytes 196640 | tf_op jit(solution)/shard_map/all_to_all | solution.py:153
  40.8 2.4 %correlate.1 = bf16[512,256]{1,0:T(8,128)(2,1)} custom-call(bf16[32,24,128]{2,1,0:T(8,128)(2,1)S(1)} %all-to-all-done.1.source_ref, bf16[16,2816]{1,0:T(8,128)(2,1)S(1)} %get-tuple-element.8.white_ref), custom_call_target="tpu_custom_call" | custom-call | tf_op jit(solution)/shard_map/correlate/pallas_call | solution.py:155
  43.2 12.7 %all-to-all-start.2 = ((bf16[16,32,256]{2,1,0:T(8,128)(2,1)}), bf16[16,32,256]{2,1,0:T(8,128)(2,1)S(1)}, u32[]{:S(2)}, u32[]{:S(2)}) async-start(bf16[16,32,256]{2,1,0:T(8,128)(2,1)} %bitcast.3), calls=%async_computation.2 | async-start | bytes 524288 | tf_op jit(solution)/shard_map/all_to_all | solution.py:170
  55.9 0.1 dynamic_slice.13
  56.0 0.1 compare_and_fusion
  56.0 15.1 %all-to-all-done.2 = bf16[16,32,256]{2,1,0:T(8,128)(2,1)S(1)} async-done(((bf16[16,32,256]{2,1,0:T(8,128)(2,1)}), bf16[16,32,256]{2,1,0:T(8,128)(2,1)S(1)}, u32[]{:S(2)}, u32[]{:S(2)}) %all-to-all-start.2) | async-done | bytes 262176 | tf_op jit(solution)/shard_map/all_to_all | solution.py:170
  71.2 0.1 mul.27
  71.4 0.1 copy.7
  71.5 0.7 broadcast_select_fusion
  (5 shorter events, 0.1 us)
Async XLA Ops:
  0.0 30.9 %copy-start = (s32[32,2]{0,1:T(2,128)S(1)}, s32[32,2]{0,1:T(2,128)}, u32[]{:S(2)}) copy-start(s32[32,2]{0,1:T(2,128)} %param.6) | copy-start | bytes 772
  0.0 0.7 copy-start.2
  0.9 0.7 copy-start.3
  2.2 0.9 %copy-start.1 = (bf16[16,8192]{1,0:T(8,128)(2,1)S(1)}, bf16[16,8192]{1,0:T(8,128)(2,1)}, u32[]{:S(2)}) copy-start(bf16[16,8192]{1,0:T(8,128)(2,1)} %record_ref.1) | copy-start | bytes 786436
  5.3 21.3 %all-to-all-start = ((bf16[32,24,128]{2,1,0:T(8,128)(2,1)}), bf16[32,24,128]{2,1,0:T(8,128)(2,1)S(1)}, u32[]{:S(2)}, u32[]{:S(2)}) async-start(bf16[32,24,128]{2,1,0:T(8,128)(2,1)} %get-tuple-element.7), calls=%async_computation | async-start | bytes 393216 | tf_op jit(solution)/shard_map/all_to_all | solution.py:144
  27.2 13.6 %all-to-all-start.1 = ((bf16[32,24,128]{2,1,0:T(8,128)(2,1)}), bf16[32,24,128]{2,1,0:T(8,128)(2,1)S(1)}, u32[]{:S(2)}, u32[]{:S(2)}) async-start(bf16[32,24,128]{2,1,0:T(8,128)(2,1)} %spread.1), calls=%async_computation.1 | async-start | bytes 393216 | tf_op jit(solution)/shard_map/all_to_all | solution.py:153
  43.2 28.0 %all-to-all-start.2 = ((bf16[16,32,256]{2,1,0:T(8,128)(2,1)}), bf16[16,32,256]{2,1,0:T(8,128)(2,1)S(1)}, u32[]{:S(2)}, u32[]{:S(2)}) async-start(bf16[16,32,256]{2,1,0:T(8,128)(2,1)} %bitcast.3), calls=%async_computation.2 | async-start | bytes 524288 | tf_op jit(solution)/shard_map/all_to_all | solution.py:170

commit v2 on v1

v2 whole, which is shorter than its diff:
```python
import functools

import jax
import jax.numpy as jnp
from jax import lax
from jax.experimental import pallas as pl
from jax.experimental.pallas import tpu as pltpu
from jax.sharding import PartitionSpec as P

WL = 2560
L = 256
SEG = WL + L
LANES = 128
TILES = SEG // LANES
BODY = WL // LANES
STEP = 16
COARSE = LANES // STEP
DEPTH = WL + LANES
EPSILON = 1e-06
CORES = 2
PLANS = ((4, 2), (6, 4), (16, 1))

VMEM = pl.BlockSpec(memory_space=pltpu.VMEM)
SMEM = pl.BlockSpec(memory_space=pltpu.SMEM)
PARAMS = pltpu.CompilerParams(vmem_limit_bytes=40 * 1024 * 1024)


def iota(shape, dim):
    return lax.broadcasted_iota(jnp.int32, shape, dim)


def column(row):
    count = row.shape[1]
    square = iota((count, count), 0) == iota((count, count), 1)
    return jnp.sum(jnp.where(square, jnp.broadcast_to(row, (count, count)), 0), axis=1, keepdims=True)


def one_hot(mask):
    return jnp.where(mask, 1.0, 0.0).astype(jnp.bfloat16)


def prepare_kernel(plan, offsets_ref, channel_ref, record_ref, white_ref, send_ref):
    slots, split = plan
    chan_dev = record_ref.shape[0]
    start = offsets_ref[lax.axis_index("src")]
    first = start // LANES
    rest = start - first * LANES
    last = record_ref.shape[1] // LANES - 1
    lane = iota((chan_dev, LANES), 1)
    shift = lax.rem(LANES - rest, LANES)

    def rolled(tile):
        at = pl.multiple_of(jnp.minimum(first + tile, last) * LANES, LANES)
        return pltpu.roll(record_ref[:, pl.ds(at, LANES)].astype(jnp.float32), shift, 1)

    segment = []
    total = jnp.zeros((chan_dev, LANES), jnp.float32)
    left = rolled(0)
    for tile in range(TILES):
        right = rolled(tile + 1)
        piece = jnp.where(lane < LANES - rest, left, right)
        segment.append(piece)
        total = total + piece * piece
        left = right
    power = jnp.sum(total, axis=1, keepdims=True) / SEG
    spread = jnp.broadcast_to(jnp.sqrt(power + EPSILON), (chan_dev, LANES))
    for tile in range(TILES):
        white_ref[:, tile * LANES : (tile + 1) * LANES] = (segment[tile] / spread).astype(jnp.bfloat16)
    base = lax.axis_index("recv") * chan_dev
    source = column(channel_ref[...])
    count = source.shape[0]
    mine = iota((count, chan_dev), 1) + base
    is_source = jnp.sum(jnp.where(source == mine, 1, 0), axis=0, keepdims=True)
    before = jnp.sum(jnp.where((source >= base) & (source < mine), 1, 0), axis=0, keepdims=True)
    row = iota((slots * split, chan_dev), 0)
    width = WL // split
    packed = None
    for part in range(split):
        pick = (before == row - part * slots) & (is_source > 0) & (row >= part * slots) & (row < (part + 1) * slots)
        term = jnp.dot(
            one_hot(pick),
            white_ref[:, L // 2 + part * width : L // 2 + (part + 1) * width],
            preferred_element_type=jnp.float32,
        )
        packed = term if packed is None else packed + term
    packed = packed.astype(jnp.bfloat16)
    for dest in range(send_ref.shape[0]):
        send_ref[dest] = packed


def shift_kernel(white_ref, shifted_ref, rows_ref):
    chan_dev = white_ref.shape[0]
    white = white_ref[...]
    for l in range(STEP):
        rows_ref[l * chan_dev : (l + 1) * chan_dev, :] = pltpu.roll(white, SEG - l, 1) if l else white
    for tile in range(TILES):
        at = slice(tile * LANES, (tile + 1) * LANES)
        shifted_ref[at, :] = rows_ref[:, at].T


def correlate_kernel(plan, channel_ref, near_ref, far_ref, shifted_ref, out_ref, a_ref, part_ref):
    slots, split = plan
    wide = shifted_ref.shape[1]
    chan_dev = wide // STEP
    count = channel_ref.shape[1]
    half = count // 2
    core = lax.rem(lax.axis_index("recv"), CORES)
    order = iota((count, count), 0)
    order = jnp.where(order < half, 2 * order, 2 * (order - half) + 1)
    every = jnp.broadcast_to(channel_ref[...], (count, count))
    source = jnp.sum(jnp.where(order == iota((count, count), 1), every, 0), axis=1, keepdims=True)
    owner = source // chan_dev
    place = jnp.sum(jnp.where((every >= owner * chan_dev) & (every < source), 1, 0), axis=1, keepdims=True)
    at = (owner // CORES) * (slots * split) + place
    is_near = lax.rem(owner, CORES) == core
    groups = near_ref.shape[0]
    total = groups * slots * split
    width = WL // split
    near = near_ref[...].reshape(total, width)
    far = far_ref[...].reshape(total, width)
    pieces = []
    for part in range(split):
        hit = iota((count, total), 1) == at + part * slots
        gathered = jnp.dot(one_hot(hit & is_near), near, preferred_element_type=jnp.float32)
        gathered = gathered + jnp.dot(one_hot(hit & ~is_near), far, preferred_element_type=jnp.float32)
        pieces.append(gathered.astype(jnp.bfloat16))
    rows = jnp.concatenate(pieces + [jnp.zeros((count, LANES), jnp.bfloat16)], axis=1)
    for m in range(COARSE):
        a_ref[m * count : (m + 1) * count, :] = pltpu.roll(rows, STEP * m, 1) if m else rows
    for high in range(L // LANES):
        product = jnp.dot(
            a_ref[...],
            shifted_ref[high * LANES : high * LANES + DEPTH, :],
            preferred_element_type=jnp.float32,
        )
        for low in range(COARSE):
            m = high * COARSE + low
            for j in range(2):
                row = low * count + j * half
                for n in range(wide // LANES):
                    part_ref[n, pl.ds(j * STEP + m, half, stride=2 * STEP), :] = product[
                        row : row + half, n * LANES : (n + 1) * LANES
                    ]
    for n in range(wide // LANES):
        out_ref[:, n * LANES : (n + 1) * LANES] = part_ref[n].astype(jnp.bfloat16)


def stack(plan, record, source_channel, band_edges, offsets):
    slots, split = plan
    chan_dev = record.shape[0]
    recv_index = lax.axis_index("recv")
    src_index = lax.axis_index("src")
    recv_count = lax.axis_size("recv")
    src_count = lax.axis_size("src")
    source_total = source_channel.shape[0]
    per = source_total // src_count
    wide = STEP * chan_dev
    groups = recv_count // CORES
    channel_row = source_channel.reshape(1, source_total)
    white, send = pl.pallas_call(
        functools.partial(prepare_kernel, plan),
        out_shape=(
            jax.ShapeDtypeStruct((chan_dev, SEG), jnp.bfloat16),
            jax.ShapeDtypeStruct((groups, slots * split, WL // split), jnp.bfloat16),
        ),
        in_specs=[SMEM, VMEM, VMEM],
        out_specs=(VMEM, VMEM),
        compiler_params=PARAMS,
        name="prepare",
    )(offsets, channel_row, record)
    near = lax.all_to_all(
        send,
        "recv",
        split_axis=0,
        concat_axis=0,
        tiled=True,
        axis_index_groups=[list(range(core, recv_count, CORES)) for core in range(CORES)],
    )
    far = lax.ppermute(near, "recv", [(i, i ^ 1) for i in range(recv_count)])
    shifted = pl.pallas_call(
        shift_kernel,
        out_shape=jax.ShapeDtypeStruct((SEG, wide), jnp.bfloat16),
        in_specs=[VMEM],
        out_specs=VMEM,
        scratch_shapes=[pltpu.VMEM((wide, SEG), jnp.bfloat16)],
        compiler_params=PARAMS,
        cost_estimate=pl.CostEstimate(flops=10**9, bytes_accessed=4 * 10**6, transcendentals=0),
        name="shift",
    )(white)
    partial = pl.pallas_call(
        functools.partial(correlate_kernel, plan),
        out_shape=jax.ShapeDtypeStruct((source_total * (L // STEP), wide), jnp.bfloat16),
        in_specs=[VMEM, VMEM, VMEM, VMEM],
        out_specs=VMEM,
        scratch_shapes=[
            pltpu.VMEM((source_total * COARSE, DEPTH), jnp.bfloat16),
            pltpu.VMEM((wide // LANES, source_total * (L // STEP), LANES), jnp.float32),
        ],
        compiler_params=PARAMS,
        name="correlate",
    )(channel_row, near, far, shifted)
    partial = partial.reshape(src_count, per * (L // STEP), wide)
    windows = lax.all_to_all(partial, "src", split_axis=0, concat_axis=0, tiled=True)
    stacked = jnp.sum(windows.astype(jnp.float32), axis=0)
    stacked = stacked.reshape(per, L // STEP, STEP, chan_dev).transpose(0, 3, 1, 2).reshape(per, chan_dev, L)
    factor = 1.0 / float(WL * src_count) ** 0.5
    own_channel = lax.dynamic_slice_in_dim(source_channel, src_index * per, per, 0)
    own_edges = lax.dynamic_slice_in_dim(band_edges, src_index * per, per, 0)
    channel_ids = recv_index * chan_dev + jnp.arange(chan_dev, dtype=jnp.int32)
    in_band = (channel_ids[None, :] >= own_edges[:, 0:1]) & (channel_ids[None, :] < own_edges[:, 1:2])
    in_band = in_band & (channel_ids[None, :] != own_channel[:, None])
    return jnp.where(in_band[:, :, None], stacked * factor, jnp.float32(0.0))


def local(record, source_channel, band_edges, offsets):
    recv_count = lax.axis_size("recv")
    owners = source_channel // record.shape[0]
    blocks = jnp.arange(recv_count, dtype=jnp.int32)
    most = jnp.max(jnp.sum((owners[None, :] == blocks[:, None]).astype(jnp.int32), axis=1))
    choice = sum((most > slots).astype(jnp.int32) for slots, _ in PLANS[:-1])
    return lax.switch(
        choice,
        [functools.partial(stack, plan) for plan in PLANS],
        record,
        source_channel,
        band_edges,
        offsets,
    )


def solution(mesh):
    in_specs = (P("recv", "src"), P(), P(), P())
    out_specs = P("src", "recv", None)
    return jax.shard_map(local, mesh=mesh, in_specs=in_specs, out_specs=out_specs, check_vma=False)
```

time: 72.6 us -> 61.9 us (0.85)
  blocking collectives: 0 us -> 21.5 us
  waiting for transfers between devices: 31.7 us -> 15 us
  starting transfers between devices: 27.7 us -> 16.5 us
  local copies, waits for them, and re-layouts: 4.08 us -> 1.02 us
  between operations: 2.68 us -> 1.31 us
  other arithmetic: 0.83 us -> 1.57 us
    all_to_all x0 -> x1, blocking collectives: none -> 21.5 us  [stack(): lax.all_to_all(send, 'recv', split_axis=0, concat_axis=0, tiled=True, axi...]
    all_to_all x3 -> x1, waiting for transfers between devices: 31.7 us -> 14.7 us  [stack(): lax.all_to_all(partial, 'src', split_axis=0, concat_axis=0, tiled=True)]
    all_to_all x3 -> x1, starting transfers between devices: 27.7 us -> 12.7 us  [stack(): lax.all_to_all(partial, 'src', split_axis=0, concat_axis=0, tiled=True)]
    ppermute x0 -> x1, starting transfers between devices: none -> 3.86 us  [stack(): far = lax.ppermute(near, 'recv', [(i, i ^ 1) for i in range(recv_count)])]
    unnamed x8 -> x2, local copies, waits for them, and re-layouts: 2.29 us -> 0.63 us
    dynamic_slice x4 -> x2, local copies, waits for them, and re-layouts: 1.33 us -> 0.16 us  [the longest x1 0.08 us: stack(): lax.dynamic_slice_in_dim(source_channel, src_index * per, per, 0)]
  transfers between devices with their start and end apart: 3 -> 2, of which waited for: 3 -> 2; matrix products, arithmetic and copies ran while one was open for 1% -> 0% of each run, Pallas kernels for 0% -> 1%
where the time goes in v2:
time: 61.9 us; the launch traced here: 61.6 us
  blocking collectives  21.5 us (35%)
  starting transfers between devices  16.5 us (27%)
  waiting for transfers between devices  15 us (24%)
  Pallas kernels  4.54 us (7%)
  other arithmetic  1.57 us (3%)
  between operations  1.31 us (2%)
  local copies, waits for them, and re-layouts  1.02 us (2%)
    all_to_all x1, blocking collectives, stack(): lax.all_to_all(send, 'recv', split_axis=0, concat_axis=0, tiled=True, axi...  21.5 us
    all_to_all x1, waiting for transfers between devices, stack(): lax.all_to_all(partial, 'src', split_axis=0, concat_axis=0, tiled=True)  14.7 us
    all_to_all x1, starting transfers between devices, stack(): lax.all_to_all(partial, 'src', split_axis=0, concat_axis=0, tiled=True)  12.7 us
    ppermute x1, starting transfers between devices, stack(): far = lax.ppermute(near, 'recv', [(i, i ^ 1) for i in range(recv_count)])  3.86 us
    pallas_call x1, Pallas kernels, stack(): pl.pallas_call(functools.partial(correlate_kernel, plan), out_shape=jax.S...  2.35 us
    pallas_call x1, Pallas kernels, stack(): pl.pallas_call(functools.partial(prepare_kernel, plan), out_shape=(jax.Sh...  1.38 us
  transfers between devices with their start and end apart: 2, of which 2 were waited for; matrix products, arithmetic and copies ran while one was open for 0% of the time, Pallas kernels for 1%

profile of v2, /device:TPU:1, one launch (start us, length us, event | category | flops | bytes accessed | tf_op | source)
XLA Modules:
  0.0 61.6 jit_solution(16519381144905352868)
XLA Ops:
  0.0 0.7 %and_select_fusion = s32[32]{0:T(128)S(1)} fusion(s32[32]{0:T(128)} %param.8), kind=kLoop, calls=%fused_computation.26 | loop fusion | flops 480 | bytes 256 | tf_op jit(solution)/shard_map/jit(floor_divide)/jit(_where)/select_n | solution.py:217
  0.7 0.1 convert_reduce_fusion.3
  0.8 0.6 %reduce_max.9 = s32[]{:T(128)} reduce(s32[32]{0:T(128)S(1)} %convert_reduce_fusion.3, s32[]{:T(128)} %constant.84.clone.1), dimensions={0}, to_apply=%region_1.2 | reduce | flops 31 | bytes 136 | tf_op jit(solution)/shard_map/reduce_max | solution.py:219
  2.7 58.2 %conditional.1 = (f32[2,16,256]{2,1,0:T(8,128)S(1)}) conditional(s32[]{:T(128)} %clamp.3, (s32[32,2]{0,1:T(2,128)}, s32[32]{0:T(128)}, s32[16]{0:T(128)}, bf16[16,8192]{1,0:T(8,128)(2,1)}) %tuple.14, (s32[32,2]{0,1:T(2,128)}, s32[32]{0:T(128)}, s32[16]{0:T(128)}, bf16[16,8192]{1,0:T(8,128)(2,1)}) %tuple.14, (s32[32,2]{0,1:T(2,128)}, ...), branch_computations={%region_2.4_spmd, %region_4.6_spmd, %region_6.8_spmd} | conditional | flops 1000270464 | bytes 13209898 | solution.py:221
  2.7 1.4 %prepare.3 = (bf16[16,2816]{1,0:T(8,128)(2,1)S(1)}, bf16[16,8,1280]{2,1,0:T(8,128)(2,1)S(1)}) custom-call(s32[16]{0:T(128)} %get-tuple-element.35.offsets_ref, s32[1,32]{1,0:T(1,128)} %bitcast.30, bf16[16,8192]{1,0:T(8,128)(2,1)} %get-tuple-element.36.record_ref), custom_call_target="tpu_custom_call" | custom-call | tf_op jit(solution)/shard_map/cond/branch_0_fun/prepare/pallas_call | solution.py:160
  4.1 21.5 %all_to_all.24.near_ref = bf16[16,8,1280]{2,1,0:T(8,128)(2,1)S(1)} all-to-all(bf16[16,8,1280]{2,1,0:T(8,128)(2,1)S(1)} %get-tuple-element.37), channel_id=1, replica_groups={{0,32,64,96,128,160,192,224,256,288,320,352,384,416,448,480},{16,48,80,..., dimensions={0} | all-to-all | bytes 655360 | tf_op jit(solution)/shard_map/cond/branch_0_fun/all_to_all | solution.py:171
  25.6 3.9 %collective-permute-start = (bf16[16,8,1280]{2,1,0:T(8,128)(2,1)S(1)}, bf16[16,8,1280]{2,1,0:T(8,128)(2,1)S(1)}, u32[]{:S(2)}, u32[]{:S(2)}) collective-permute-start(bf16[16,8,1280]{2,1,0:T(8,128)(2,1)S(1)} %all_to_all.24.near_ref), channel_id=1, source_target_pairs={{0,16},{16,0},{32,48},{48,32},{64,80},{80,64},{96,112},{112,96},{1... | collective-permute-start | bytes 983048 | tf_op jit(solution)/shard_map/cond/branch_0_fun/ppermute | solution.py:179
  29.5 0.0 copy-start.4
  29.5 0.0 copy-start.1
  29.5 0.8 %shift.3.shifted_ref = bf16[2816,256]{1,0:T(8,128)(2,1)S(1)} custom-call(bf16[16,2816]{1,0:T(8,128)(2,1)S(1)} %get-tuple-element.38.white_ref), custom_call_target="tpu_custom_call" | custom-call | flops 1000000000 | bytes 4000000 | tf_op jit(solution)/shard_map/cond/branch_0_fun/shift/pallas_call | solution.py:180
  30.3 0.0 copy-done.4
  30.3 0.1 constant_dynamic-slice_fusion
  30.4 0.3 collective-permute-done.far_ref
  30.7 0.0 copy-done.1
  30.7 2.4 %correlate.3 = bf16[512,256]{1,0:T(8,128)(2,1)} custom-call(s32[1,32]{1,0:T(1,128)S(1)} %bitcast.31, bf16[16,8,1280]{2,1,0:T(8,128)(2,1)S(1)} %all_to_all.24.near_ref, bf16[16,8,1280]{2,1,0:T(8,128)(2,1)S(1)} %collective-permute-done.far_ref, bf16[2816,256]{1,0:T(8,128)(2,1)S(1)} %shift.3.shifted_ref), custom_call_target="tpu_custom_call" | custom-call | tf_op jit(solution)/shard_map/cond/branch_0_fun/correlate/pallas_call | solution.py:190
  33.0 12.7 %all-to-all-start.1 = ((bf16[16,32,256]{2,1,0:T(8,128)(2,1)}), bf16[16,32,256]{2,1,0:T(8,128)(2,1)S(1)}, u32[]{:S(2)}, u32[]{:S(2)}) async-start(bf16[16,32,256]{2,1,0:T(8,128)(2,1)} %bitcast.3), calls=%async_computation.1 | async-start | bytes 524288 | tf_op jit(solution)/shard_map/cond/branch_0_fun/all_to_all | solution.py:203
  45.7 0.1 dynamic_slice.13
  45.8 0.1 compare_and_fusion
  45.9 14.7 %all-to-all-done.1 = bf16[16,32,256]{2,1,0:T(8,128)(2,1)S(1)} async-done(((bf16[16,32,256]{2,1,0:T(8,128)(2,1)}), bf16[16,32,256]{2,1,0:T(8,128)(2,1)S(1)}, u32[]{:S(2)}, u32[]{:S(2)}) %all-to-all-start.1) | async-done | bytes 262176 | tf_op jit(solution)/shard_map/cond/branch_0_fun/all_to_all | solution.py:203
  60.7 0.1 mul.42
  60.8 0.1 copy.10
  60.9 0.0 copy-start
  60.9 0.6 %copy-done = f32[2,16,256]{2,1,0:T(8,128)} copy-done((f32[2,16,256]{2,1,0:T(8,128)}, f32[2,16,256]{2,1,0:T(8,128)S(1)}, u32[]{:S(2)}) %copy-start) | copy-done | bytes 32792
  (5 shorter events, 0.1 us)
Async XLA Ops:
  25.6 5.1 %collective-permute-start = (bf16[16,8,1280]{2,1,0:T(8,128)(2,1)S(1)}, bf16[16,8,1280]{2,1,0:T(8,128)(2,1)S(1)}, u32[]{:S(2)}, u32[]{:S(2)}) collective-permute-start(bf16[16,8,1280]{2,1,0:T(8,128)(2,1)S(1)} %all_to_all.24.near_ref), channel_id=1, source_target_pairs={{0,16},{16,0},{32,48},{48,32},{64,80},{80,64},{96,112},{112,96},{1... | collective-permute-start | bytes 983048 | tf_op jit(solution)/shard_map/cond/branch_0_fun/ppermute | solution.py:179
  29.5 0.8 %copy-start.4 = (s32[32,2]{0,1:T(2,128)S(1)}, s32[32,2]{0,1:T(2,128)}, u32[]{:S(2)}) copy-start(s32[32,2]{0,1:T(2,128)} %get-tuple-element.32) | copy-start | bytes 772 | tf_op jit(solution)/shard_map/cond
  29.5 1.2 %copy-start.1 = (s32[32]{0:T(128)S(1)}, s32[32]{0:T(128)}, u32[]{:S(2)}) copy-start(s32[32]{0:T(128)} %get-tuple-element.34) | copy-start | bytes 388 | tf_op jit(solution)/shard_map/cond
  33.0 27.6 %all-to-all-start.1 = ((bf16[16,32,256]{2,1,0:T(8,128)(2,1)}), bf16[16,32,256]{2,1,0:T(8,128)(2,1)S(1)}, u32[]{:S(2)}, u32[]{:S(2)}) async-start(bf16[16,32,256]{2,1,0:T(8,128)(2,1)} %bitcast.3), calls=%async_computation.1 | async-start | bytes 524288 | tf_op jit(solution)/shard_map/cond/branch_0_fun/all_to_all | solution.py:203
  60.9 0.6 %copy-start = (f32[2,16,256]{2,1,0:T(8,128)}, f32[2,16,256]{2,1,0:T(8,128)S(1)}, u32[]{:S(2)}) copy-start(f32[2,16,256]{2,1,0:T(8,128)S(1)} %get-tuple-element.71) | copy-start | bytes 98308

commit v3 on v2

--- a/solution.py
+++ b/solution.py
@@ -18,7 +18,7 @@
 DEPTH = WL + LANES
 EPSILON = 1e-06
 CORES = 2
-PLANS = ((4, 2), (6, 4), (16, 1))
+PLANS = ((3, 5, 16), (4, 2, 8), (6, 4, 24), (16, 1, 16))
 
 VMEM = pl.BlockSpec(memory_space=pltpu.VMEM)
 SMEM = pl.BlockSpec(memory_space=pltpu.SMEM)
@@ -40,7 +40,7 @@
 
 
 def prepare_kernel(plan, offsets_ref, channel_ref, record_ref, white_ref, send_ref):
-    slots, split = plan
+    slots, split, rows = plan
     chan_dev = record_ref.shape[0]
     start = offsets_ref[lax.axis_index("src")]
     first = start // LANES
@@ -68,11 +68,10 @@
         white_ref[:, tile * LANES : (tile + 1) * LANES] = (segment[tile] / spread).astype(jnp.bfloat16)
     base = lax.axis_index("recv") * chan_dev
     source = column(channel_ref[...])
-    count = source.shape[0]
-    mine = iota((count, chan_dev), 1) + base
+    mine = iota((source.shape[0], chan_dev), 1) + base
     is_source = jnp.sum(jnp.where(source == mine, 1, 0), axis=0, keepdims=True)
     before = jnp.sum(jnp.where((source >= base) & (source < mine), 1, 0), axis=0, keepdims=True)
-    row = iota((slots * split, chan_dev), 0)
+    row = iota((rows, chan_dev), 0)
     width = WL // split
     packed = None
     for part in range(split):
@@ -99,7 +98,7 @@
 
 
 def correlate_kernel(plan, channel_ref, near_ref, far_ref, shifted_ref, out_ref, a_ref, part_ref):
-    slots, split = plan
+    slots, split, rows = plan
     wide = shifted_ref.shape[1]
     chan_dev = wide // STEP
     count = channel_ref.shape[1]
@@ -111,10 +110,10 @@
     source = jnp.sum(jnp.where(order == iota((count, count), 1), every, 0), axis=1, keepdims=True)
     owner = source // chan_dev
     place = jnp.sum(jnp.where((every >= owner * chan_dev) & (every < source), 1, 0), axis=1, keepdims=True)
-    at = (owner // CORES) * (slots * split) + place
+    at = (owner // CORES) * rows + place
     is_near = lax.rem(owner, CORES) == core
     groups = near_ref.shape[0]
-    total = groups * slots * split
+    total = groups * rows
     width = WL // split
     near = near_ref[...].reshape(total, width)
     far = far_ref[...].reshape(total, width)
@@ -124,9 +123,9 @@
         gathered = jnp.dot(one_hot(hit & is_near), near, preferred_element_type=jnp.float32)
         gathered = gathered + jnp.dot(one_hot(hit & ~is_near), far, preferred_element_type=jnp.float32)
         pieces.append(gathered.astype(jnp.bfloat16))
-    rows = jnp.concatenate(pieces + [jnp.zeros((count, LANES), jnp.bfloat16)], axis=1)
+    joined = jnp.concatenate(pieces + [jnp.zeros((count, LANES), jnp.bfloat16)], axis=1)
     for m in range(COARSE):
-        a_ref[m * count : (m + 1) * count, :] = pltpu.roll(rows, STEP * m, 1) if m else rows
+        a_ref[m * count : (m + 1) * count, :] = pltpu.roll(joined, STEP * m, 1) if m else joined
     for high in range(L // LANES):
         product = jnp.dot(
             a_ref[...],
@@ -146,7 +145,7 @@
 
 
 def stack(plan, record, source_channel, band_edges, offsets):
-    slots, split = plan
+    slots, split, rows = plan
     chan_dev = record.shape[0]
     recv_index = lax.axis_index("recv")
     src_index = lax.axis_index("src")
@@ -161,7 +160,7 @@
         functools.partial(prepare_kernel, plan),
         out_shape=(
             jax.ShapeDtypeStruct((chan_dev, SEG), jnp.bfloat16),
-            jax.ShapeDtypeStruct((groups, slots * split, WL // split), jnp.bfloat16),
+            jax.ShapeDtypeStruct((groups, rows, WL // split), jnp.bfloat16),
         ),
         in_specs=[SMEM, VMEM, VMEM],
         out_specs=(VMEM, VMEM),
@@ -213,11 +212,10 @@
 
 
 def local(record, source_channel, band_edges, offsets):
-    recv_count = lax.axis_size("recv")
+    blocks = jnp.arange(lax.axis_size("recv"), dtype=jnp.int32)
     owners = source_channel // record.shape[0]
-    blocks = jnp.arange(recv_count, dtype=jnp.int32)
-    most = jnp.max(jnp.sum((owners[None, :] == blocks[:, None]).astype(jnp.int32), axis=1))
-    choice = sum((most > slots).astype(jnp.int32) for slots, _ in PLANS[:-1])
+    held = jnp.sum((owners[None, :] == blocks[:, None]).astype(jnp.int32), axis=1)
+    choice = jnp.max(sum((held > plan[0]).astype(jnp.int32) for plan in PLANS[:-1]))
     return lax.switch(
         choice,
         [functools.partial(stack, plan) for plan in PLANS],

time: 61.9 us -> 60.1 us (0.971)
  blocking collectives: 21.5 us -> 19.9 us
  between operations: 1.31 us -> 0.67 us
    all_to_all x1, blocking collectives: 21.5 us -> 19.9 us  [stack(): lax.all_to_all(send, 'recv', split_axis=0, concat_axis=0, tiled=True, axi...]
where the time goes in v3:
time: 60.1 us; the launch traced here: 59.8 us
  blocking collectives  19.9 us (33%)
  starting transfers between devices  16.7 us (28%)
  waiting for transfers between devices  14.9 us (25%)
  Pallas kernels  4.73 us (8%)
  other arithmetic  1.57 us (3%)
  local copies, waits for them, and re-layouts  1 us (2%)
  between operations  0.67 us (1%)
    all_to_all x1, blocking collectives, stack(): lax.all_to_all(send, 'recv', split_axis=0, concat_axis=0, tiled=True, axi...  19.9 us
    all_to_all x1, waiting for transfers between devices, stack(): lax.all_to_all(partial, 'src', split_axis=0, concat_axis=0, tiled=True)  14.7 us
    all_to_all x1, starting transfers between devices, stack(): lax.all_to_all(partial, 'src', split_axis=0, concat_axis=0, tiled=True)  12.7 us
    ppermute x1, starting transfers between devices, stack(): far = lax.ppermute(near, 'recv', [(i, i ^ 1) for i in range(recv_count)])  4.05 us
    pallas_call x1, Pallas kernels, stack(): pl.pallas_call(functools.partial(correlate_kernel, plan), out_shape=jax.S...  2.54 us
    pallas_call x1, Pallas kernels, stack(): pl.pallas_call(functools.partial(prepare_kernel, plan), out_shape=(jax.Sh...  1.38 us
  transfers between devices with their start and end apart: 2, of which 2 were waited for; matrix products, arithmetic and copies ran while one was open for 0% of the time, Pallas kernels for 1%

profile of v3, /device:TPU:1, one launch (start us, length us, event | category | flops | bytes accessed | tf_op | source)
XLA Modules:
  0.0 59.8 jit_solution(10141709773866735892)
XLA Ops:
  0.0 0.7 %and_select_fusion = s32[32]{0:T(128)S(1)} fusion(s32[32]{0:T(128)} %param.9), kind=kLoop, calls=%fused_computation.37 | loop fusion | flops 480 | bytes 256 | tf_op jit(solution)/shard_map/jit(floor_divide)/jit(_where)/select_n | solution.py:216
  0.7 0.1 convert_reduce_fusion.4
  0.8 0.6 %fusion.2 = s32[]{:T(128)} fusion(s32[32]{0:T(128)S(1)} %convert_reduce_fusion.4), kind=kLoop, calls=%fused_computation.43 | loop fusion | flops 287 | bytes 132 | tf_op jit(solution)/shard_map/reduce_max | solution.py:218
  2.1 57.1 %conditional.1 = (f32[2,16,256]{2,1,0:T(8,128)S(1)}) conditional(s32[]{:T(128)} %clamp.3, (s32[32,2]{0,1:T(2,128)}, s32[32]{0:T(128)}, s32[16]{0:T(128)}, bf16[16,8192]{1,0:T(8,128)(2,1)}) %tuple.17, (s32[32,2]{0,1:T(2,128)}, s32[32]{0:T(128)}, s32[16]{0:T(128)}, bf16[16,8192]{1,0:T(8,128)(2,1)}) %tuple.17, ...), branch_computations={%region_2.4_spmd, %region_4.6_spmd, %region_6.8_spmd, %region_8.10... | conditional | flops 1000270464 | bytes 13209898 | solution.py:219
  2.1 1.4 %prepare.4 = (bf16[16,2816]{1,0:T(8,128)(2,1)S(1)}, bf16[16,16,512]{2,1,0:T(8,128)(2,1)S(1)}) custom-call(s32[16]{0:T(128)} %get-tuple-element.44.offsets_ref, s32[1,32]{1,0:T(1,128)} %bitcast.40, bf16[16,8192]{1,0:T(8,128)(2,1)} %get-tuple-element.45.record_ref), custom_call_target="tpu_custom_call" | custom-call | tf_op jit(solution)/shard_map/cond/branch_0_fun/prepare/pallas_call | solution.py:159
  3.5 19.9 %all_to_all.32.near_ref = bf16[16,16,512]{2,1,0:T(8,128)(2,1)S(1)} all-to-all(bf16[16,16,512]{2,1,0:T(8,128)(2,1)S(1)} %get-tuple-element.46), channel_id=1, replica_groups={{0,32,64,96,128,160,192,224,256,288,320,352,384,416,448,480},{16,48,80,..., dimensions={0} | all-to-all | bytes 524288 | tf_op jit(solution)/shard_map/cond/branch_0_fun/all_to_all | solution.py:170
  23.4 4.0 %collective-permute-start = (bf16[16,16,512]{2,1,0:T(8,128)(2,1)S(1)}, bf16[16,16,512]{2,1,0:T(8,128)(2,1)S(1)}, u32[]{:S(2)}, u32[]{:S(2)}) collective-permute-start(bf16[16,16,512]{2,1,0:T(8,128)(2,1)S(1)} %all_to_all.32.near_ref), channel_id=1, source_target_pairs={{0,16},{16,0},{32,48},{48,32},{64,80},{80,64},{96,112},{112,96},{1... | collective-permute-start | bytes 786440 | tf_op jit(solution)/shard_map/cond/branch_0_fun/ppermute | solution.py:178
  27.4 0.0 copy-start.5
  27.4 0.0 copy-start
  27.4 0.8 %shift.4.shifted_ref = bf16[2816,256]{1,0:T(8,128)(2,1)S(1)} custom-call(bf16[16,2816]{1,0:T(8,128)(2,1)S(1)} %get-tuple-element.47.white_ref), custom_call_target="tpu_custom_call" | custom-call | flops 1000000000 | bytes 4000000 | tf_op jit(solution)/shard_map/cond/branch_0_fun/shift/pallas_call | solution.py:179
  28.3 0.0 copy-done.5
  28.3 0.1 constant_dynamic-slice_fusion
  28.3 0.2 collective-permute-done.far_ref
  28.5 0.0 copy-done
  28.6 2.5 %correlate.4 = bf16[512,256]{1,0:T(8,128)(2,1)} custom-call(s32[1,32]{1,0:T(1,128)S(1)} %bitcast.41, bf16[16,16,512]{2,1,0:T(8,128)(2,1)S(1)} %all_to_all.32.near_ref, bf16[16,16,512]{2,1,0:T(8,128)(2,1)S(1)} %collective-permute-done.far_ref, bf16[2816,256]{1,0:T(8,128)(2,1)S(1)} %shift.4.shifted_ref), custom_call_target="tpu_custom_call" | custom-call | tf_op jit(solution)/shard_map/cond/branch_0_fun/correlate/pallas_call | solution.py:189
  31.1 12.7 %all-to-all-start.1 = ((bf16[16,32,256]{2,1,0:T(8,128)(2,1)}), bf16[16,32,256]{2,1,0:T(8,128)(2,1)S(1)}, u32[]{:S(2)}, u32[]{:S(2)}) async-start(bf16[16,32,256]{2,1,0:T(8,128)(2,1)} %bitcast.3), calls=%async_computation.1 | async-start | bytes 524288 | tf_op jit(solution)/shard_map/cond/branch_0_fun/all_to_all | solution.py:202
  43.8 0.1 dynamic_slice.17
  43.9 0.1 compare_and_fusion
  43.9 14.7 %all-to-all-done.1 = bf16[16,32,256]{2,1,0:T(8,128)(2,1)S(1)} async-done(((bf16[16,32,256]{2,1,0:T(8,128)(2,1)}), bf16[16,32,256]{2,1,0:T(8,128)(2,1)S(1)}, u32[]{:S(2)}, u32[]{:S(2)}) %all-to-all-start.1) | async-done | bytes 262176 | tf_op jit(solution)/shard_map/cond/branch_0_fun/all_to_all | solution.py:202
  58.7 0.1 mul.55
  58.9 0.1 copy.11
  59.2 0.0 copy-start.4
  59.2 0.6 %copy-done.4 = f32[2,16,256]{2,1,0:T(8,128)} copy-done((f32[2,16,256]{2,1,0:T(8,128)}, f32[2,16,256]{2,1,0:T(8,128)S(1)}, u32[]{:S(2)}) %copy-start.4) | copy-done | bytes 32792
  (5 shorter events, 0.1 us)
Async XLA Ops:
  23.4 5.2 %collective-permute-start = (bf16[16,16,512]{2,1,0:T(8,128)(2,1)S(1)}, bf16[16,16,512]{2,1,0:T(8,128)(2,1)S(1)}, u32[]{:S(2)}, u32[]{:S(2)}) collective-permute-start(bf16[16,16,512]{2,1,0:T(8,128)(2,1)S(1)} %all_to_all.32.near_ref), channel_id=1, source_target_pairs={{0,16},{16,0},{32,48},{48,32},{64,80},{80,64},{96,112},{112,96},{1... | collective-permute-start | bytes 786440 | tf_op jit(solution)/shard_map/cond/branch_0_fun/ppermute | solution.py:178
  27.4 0.8 %copy-start.5 = (s32[32,2]{0,1:T(2,128)S(1)}, s32[32,2]{0,1:T(2,128)}, u32[]{:S(2)}) copy-start(s32[32,2]{0,1:T(2,128)} %get-tuple-element.40) | copy-start | bytes 772 | tf_op jit(solution)/shard_map/cond
  27.4 1.1 %copy-start = (s32[32]{0:T(128)S(1)}, s32[32]{0:T(128)}, u32[]{:S(2)}) copy-start(s32[32]{0:T(128)} %get-tuple-element.42) | copy-start | bytes 388 | tf_op jit(solution)/shard_map/cond
  31.1 27.6 %all-to-all-start.1 = ((bf16[16,32,256]{2,1,0:T(8,128)(2,1)}), bf16[16,32,256]{2,1,0:T(8,128)(2,1)S(1)}, u32[]{:S(2)}, u32[]{:S(2)}) async-start(bf16[16,32,256]{2,1,0:T(8,128)(2,1)} %bitcast.3), calls=%async_computation.1 | async-start | bytes 524288 | tf_op jit(solution)/shard_map/cond/branch_0_fun/all_to_all | solution.py:202
  59.2 0.6 %copy-start.4 = (f32[2,16,256]{2,1,0:T(8,128)}, f32[2,16,256]{2,1,0:T(8,128)S(1)}, u32[]{:S(2)}) copy-start(f32[2,16,256]{2,1,0:T(8,128)S(1)} %get-tuple-element.92) | copy-start | bytes 98308

commit v4 on v3

--- a/solution.py
+++ b/solution.py
@@ -111,18 +111,14 @@
     owner = source // chan_dev
     place = jnp.sum(jnp.where((every >= owner * chan_dev) & (every < source), 1, 0), axis=1, keepdims=True)
     at = (owner // CORES) * rows + place
-    is_near = lax.rem(owner, CORES) == core
     groups = near_ref.shape[0]
     total = groups * rows
     width = WL // split
-    near = near_ref[...].reshape(total, width)
-    far = far_ref[...].reshape(total, width)
-    pieces = []
-    for part in range(split):
-        hit = iota((count, total), 1) == at + part * slots
-        gathered = jnp.dot(one_hot(hit & is_near), near, preferred_element_type=jnp.float32)
-        gathered = gathered + jnp.dot(one_hot(hit & ~is_near), far, preferred_element_type=jnp.float32)
-        pieces.append(gathered.astype(jnp.bfloat16))
+    both = jnp.concatenate([near_ref[...].reshape(total, width), far_ref[...].reshape(total, width)], axis=0)
+    at = jnp.where(lax.rem(owner, CORES) == core, at, at + total)
+    hits = [one_hot(iota((count, CORES * total), 1) == at + part * slots) for part in range(split)]
+    gathered = jnp.dot(jnp.concatenate(hits, axis=0), both, preferred_element_type=jnp.float32).astype(jnp.bfloat16)
+    pieces = [gathered[part * count : (part + 1) * count] for part in range(split)]
     joined = jnp.concatenate(pieces + [jnp.zeros((count, LANES), jnp.bfloat16)], axis=1)
     for m in range(COARSE):
         a_ref[m * count : (m + 1) * count, :] = pltpu.roll(joined, STEP * m, 1) if m else joined
@@ -154,13 +150,12 @@
     source_total = source_channel.shape[0]
     per = source_total // src_count
     wide = STEP * chan_dev
-    groups = recv_count // CORES
     channel_row = source_channel.reshape(1, source_total)
     white, send = pl.pallas_call(
         functools.partial(prepare_kernel, plan),
         out_shape=(
             jax.ShapeDtypeStruct((chan_dev, SEG), jnp.bfloat16),
-            jax.ShapeDtypeStruct((groups, rows, WL // split), jnp.bfloat16),
+            jax.ShapeDtypeStruct((recv_count // CORES, rows, WL // split), jnp.bfloat16),
         ),
         in_specs=[SMEM, VMEM, VMEM],
         out_specs=(VMEM, VMEM),
@@ -176,6 +171,12 @@
         axis_index_groups=[list(range(core, recv_count, CORES)) for core in range(CORES)],
     )
     far = lax.ppermute(near, "recv", [(i, i ^ 1) for i in range(recv_count)])
+    far, source_channel, band_edges = lax.optimization_barrier((far, source_channel, band_edges))
+    own_channel = lax.dynamic_slice_in_dim(source_channel, src_index * per, per, 0)
+    own_edges = lax.dynamic_slice_in_dim(band_edges, src_index * per, per, 0)
+    channel_ids = recv_index * chan_dev + jnp.arange(chan_dev, dtype=jnp.int32)
+    keep = (channel_ids[None, :] >= own_edges[:, 0:1]) & (channel_ids[None, :] < own_edges[:, 1:2])
+    keep = keep & (channel_ids[None, :] != own_channel[:, None])
     shifted = pl.pallas_call(
         shift_kernel,
         out_shape=jax.ShapeDtypeStruct((SEG, wide), jnp.bfloat16),
@@ -198,17 +199,13 @@
         compiler_params=PARAMS,
         name="correlate",
     )(channel_row, near, far, shifted)
+    partial, keep = lax.optimization_barrier((partial, keep))
     partial = partial.reshape(src_count, per * (L // STEP), wide)
     windows = lax.all_to_all(partial, "src", split_axis=0, concat_axis=0, tiled=True)
     stacked = jnp.sum(windows.astype(jnp.float32), axis=0)
     stacked = stacked.reshape(per, L // STEP, STEP, chan_dev).transpose(0, 3, 1, 2).reshape(per, chan_dev, L)
     factor = 1.0 / float(WL * src_count) ** 0.5
-    own_channel = lax.dynamic_slice_in_dim(source_channel, src_index * per, per, 0)
-    own_edges = lax.dynamic_slice_in_dim(band_edges, src_index * per, per, 0)
-    channel_ids = recv_index * chan_dev + jnp.arange(chan_dev, dtype=jnp.int32)
-    in_band = (channel_ids[None, :] >= own_edges[:, 0:1]) & (channel_ids[None, :] < own_edges[:, 1:2])
-    in_band = in_band & (channel_ids[None, :] != own_channel[:, None])
-    return jnp.where(in_band[:, :, None], stacked * factor, jnp.float32(0.0))
+    return jnp.where(keep[:, :, None], stacked * factor, jnp.float32(0.0))
 
 
 def local(record, source_channel, band_edges, offsets):

time: 60.1 us -> 59.2 us (0.985)
  blocking collectives: 19.9 us -> 47.2 us
  waiting for transfers between devices: 14.9 us -> 0.28 us
  starting transfers between devices: 16.7 us -> 4.05 us
  Pallas kernels: 4.73 us -> 3.85 us
    all_to_all x0 -> x1, blocking collectives: none -> 27.4 us  [stack(): lax.all_to_all(partial, 'src', split_axis=0, concat_axis=0, tiled=True)]
    all_to_all x1 -> x0, waiting for transfers between devices: 14.7 us -> none  [stack(): lax.all_to_all(partial, 'src', split_axis=0, concat_axis=0, tiled=True)]
    all_to_all x1 -> x0, starting transfers between devices: 12.7 us -> none  [stack(): lax.all_to_all(partial, 'src', split_axis=0, concat_axis=0, tiled=True)]
    pallas_call x1, Pallas kernels: 2.54 us -> 1.65 us  [stack(): pl.pallas_call(functools.partial(correlate_kernel, plan), out_shape=jax.S...]
  transfers between devices with their start and end apart: 2 -> 1, of which waited for: 2 -> 1; matrix products, arithmetic and copies ran while one was open for 0% -> 0% of each run, Pallas kernels for 1% -> 1%
where the time goes in v4:
time: 59.2 us; the launch traced here: 59 us
  blocking collectives  47.2 us (80%)
  starting transfers between devices  4.05 us (7%)
  Pallas kernels  3.85 us (7%)
  other arithmetic  1.57 us (3%)
  local copies, waits for them, and re-layouts  0.99 us (2%)
  between operations  0.67 us (1%)
    all_to_all x1, blocking collectives, stack(): lax.all_to_all(partial, 'src', split_axis=0, concat_axis=0, tiled=True)  27.4 us
    all_to_all x1, blocking collectives, stack(): lax.all_to_all(send, 'recv', split_axis=0, concat_axis=0, tiled=True, axi...  19.9 us
    ppermute x1, starting transfers between devices, stack(): far = lax.ppermute(near, 'recv', [(i, i ^ 1) for i in range(recv_count)])  4.05 us
    pallas_call x1, Pallas kernels, stack(): pl.pallas_call(functools.partial(correlate_kernel, plan), out_shape=jax.S...  1.65 us
    pallas_call x1, Pallas kernels, stack(): pl.pallas_call(functools.partial(prepare_kernel, plan), out_shape=(jax.Sh...  1.38 us
  transfers between devices with their start and end apart: 1, of which 1 were waited for; matrix products, arithmetic and copies ran while one was open for 0% of the time, Pallas kernels for 1%

profile of v4, /device:TPU:1, one launch (start us, length us, event | category | flops | bytes accessed | tf_op | source)
XLA Modules:
  0.0 59.0 jit_solution(17999918159608695229)
XLA Ops:
  0.0 0.7 %and_select_fusion = s32[32]{0:T(128)S(1)} fusion(s32[32]{0:T(128)} %param.9), kind=kLoop, calls=%fused_computation.37 | loop fusion | flops 480 | bytes 256 | tf_op jit(solution)/shard_map/jit(floor_divide)/jit(_where)/select_n | solution.py:213
  0.7 0.1 convert_reduce_fusion.4
  0.8 0.6 %fusion.2 = s32[]{:T(128)} fusion(s32[32]{0:T(128)S(1)} %convert_reduce_fusion.4), kind=kLoop, calls=%fused_computation.43 | loop fusion | flops 287 | bytes 132 | tf_op jit(solution)/shard_map/reduce_max | solution.py:215
  2.1 56.3 %conditional.1 = (f32[2,16,256]{2,1,0:T(8,128)S(1)}) conditional(s32[]{:T(128)} %clamp.3, (s32[32]{0:T(128)}, s32[16]{0:T(128)}, bf16[16,8192]{1,0:T(8,128)(2,1)}, s32[32,2]{0,1:T(2,128)}) %tuple.25, (s32[32]{0:T(128)}, s32[16]{0:T(128)}, bf16[16,8192]{1,0:T(8,128)(2,1)}, s32[32,2]{0,1:T(2,128)}) %tuple.25, ...), branch_computations={%region_2.4_spmd, %region_4.6_spmd, %region_6.8_spmd, %region_8.10... | conditional | flops 1000270464 | bytes 12947722 | solution.py:216
  2.1 1.4 %prepare.4 = (bf16[16,2816]{1,0:T(8,128)(2,1)S(1)}, bf16[16,16,512]{2,1,0:T(8,128)(2,1)S(1)}) custom-call(s32[16]{0:T(128)} %get-tuple-element.42.offsets_ref, s32[1,32]{1,0:T(1,128)} %bitcast.44, bf16[16,8192]{1,0:T(8,128)(2,1)} %get-tuple-element.44.record_ref), custom_call_target="tpu_custom_call" | custom-call | tf_op jit(solution)/shard_map/cond/branch_0_fun/prepare/pallas_call | solution.py:154
  3.5 19.9 %all_to_all.32.near_ref = bf16[16,16,512]{2,1,0:T(8,128)(2,1)S(1)} all-to-all(bf16[16,16,512]{2,1,0:T(8,128)(2,1)S(1)} %get-tuple-element.45), channel_id=1, replica_groups={{0,32,64,96,128,160,192,224,256,288,320,352,384,416,448,480},{16,48,80,..., dimensions={0} | all-to-all | bytes 524288 | tf_op jit(solution)/shard_map/cond/branch_0_fun/all_to_all | solution.py:165
  23.4 4.0 %collective-permute-start = (bf16[16,16,512]{2,1,0:T(8,128)(2,1)S(1)}, bf16[16,16,512]{2,1,0:T(8,128)(2,1)S(1)}, u32[]{:S(2)}, u32[]{:S(2)}) collective-permute-start(bf16[16,16,512]{2,1,0:T(8,128)(2,1)S(1)} %all_to_all.32.near_ref), channel_id=1, source_target_pairs={{0,16},{16,0},{32,48},{48,32},{64,80},{80,64},{96,112},{112,96},{1... | collective-permute-start | bytes 786440 | tf_op jit(solution)/shard_map/cond/branch_0_fun/ppermute | solution.py:173
  27.4 0.0 copy-start
  27.4 0.0 copy-start.5
  27.4 0.8 %shift.4.shifted_ref = bf16[2816,256]{1,0:T(8,128)(2,1)S(1)} custom-call(bf16[16,2816]{1,0:T(8,128)(2,1)S(1)} %get-tuple-element.48.white_ref), custom_call_target="tpu_custom_call" | custom-call | flops 1000000000 | bytes 4000000 | tf_op jit(solution)/shard_map/cond/branch_0_fun/shift/pallas_call | solution.py:180
  28.3 0.3 collective-permute-done.far_ref
  28.5 0.0 copy-done
  28.6 0.1 dynamic_slice.17
  28.6 0.0 copy-done.5
  28.6 0.1 constant_dynamic-slice_fusion
  28.7 0.1 compare_and_fusion
  28.8 1.7 %correlate.4 = bf16[512,256]{1,0:T(8,128)(2,1)S(1)} custom-call(s32[1,32]{1,0:T(1,128)S(1)} %bitcast.45, bf16[16,16,512]{2,1,0:T(8,128)(2,1)S(1)} %all_to_all.32.near_ref, bf16[16,16,512]{2,1,0:T(8,128)(2,1)S(1)} %collective-permute-done.far_ref, bf16[2816,256]{1,0:T(8,128)(2,1)S(1)} %shift.4.shifted_ref), custom_call_target="tpu_custom_call" | custom-call | tf_op jit(solution)/shard_map/cond/branch_0_fun/correlate/pallas_call | solution.py:190
  30.4 27.4 %all_to_all.33 = bf16[16,32,256]{2,1,0:T(8,128)(2,1)S(1)} all-to-all(bf16[16,32,256]{2,1,0:T(8,128)(2,1)S(1)} %bitcast.40), channel_id=1, replica_groups=mesh['recv'=32,'src'=16] {'src'}, dimensions={0} | all-to-all | bytes 524288 | tf_op jit(solution)/shard_map/cond/branch_0_fun/all_to_all | solution.py:204
  57.9 0.1 mul.55
  58.0 0.1 copy.11
  58.3 0.0 copy-start.4
  58.4 0.6 %copy-done.4 = f32[2,16,256]{2,1,0:T(8,128)} copy-done((f32[2,16,256]{2,1,0:T(8,128)}, f32[2,16,256]{2,1,0:T(8,128)S(1)}, u32[]{:S(2)}) %copy-start.4) | copy-done | bytes 32792
  (5 shorter events, 0.1 us)
Async XLA Ops:
  23.4 5.2 %collective-permute-start = (bf16[16,16,512]{2,1,0:T(8,128)(2,1)S(1)}, bf16[16,16,512]{2,1,0:T(8,128)(2,1)S(1)}, u32[]{:S(2)}, u32[]{:S(2)}) collective-permute-start(bf16[16,16,512]{2,1,0:T(8,128)(2,1)S(1)} %all_to_all.32.near_ref), channel_id=1, source_target_pairs={{0,16},{16,0},{32,48},{48,32},{64,80},{80,64},{96,112},{112,96},{1... | collective-permute-start | bytes 786440 | tf_op jit(solution)/shard_map/cond/branch_0_fun/ppermute | solution.py:173
  27.4 1.1 %copy-start = (s32[32]{0:T(128)S(1)}, s32[32]{0:T(128)}, u32[]{:S(2)}) copy-start(s32[32]{0:T(128)} %get-tuple-element.50) | copy-start | bytes 388 | tf_op jit(solution)/shard_map/cond
  27.4 1.2 %copy-start.5 = (s32[32,2]{0,1:T(2,128)S(1)}, s32[32,2]{0,1:T(2,128)}, u32[]{:S(2)}) copy-start(s32[32,2]{0,1:T(2,128)} %get-tuple-element.49) | copy-start | bytes 772 | tf_op jit(solution)/shard_map/cond
  58.3 0.6 %copy-start.4 = (f32[2,16,256]{2,1,0:T(8,128)}, f32[2,16,256]{2,1,0:T(8,128)S(1)}, u32[]{:S(2)}) copy-start(f32[2,16,256]{2,1,0:T(8,128)S(1)} %get-tuple-element.108) | copy-start | bytes 98308

commit v5 on v4

--- a/solution.py
+++ b/solution.py
@@ -23,6 +23,7 @@
 VMEM = pl.BlockSpec(memory_space=pltpu.VMEM)
 SMEM = pl.BlockSpec(memory_space=pltpu.SMEM)
 PARAMS = pltpu.CompilerParams(vmem_limit_bytes=40 * 1024 * 1024)
+EARLY = 2
 
 
 def iota(shape, dim):
@@ -39,9 +40,27 @@
     return jnp.where(mask, 1.0, 0.0).astype(jnp.bfloat16)
 
 
-def prepare_kernel(plan, offsets_ref, channel_ref, record_ref, white_ref, send_ref):
-    slots, split, rows = plan
+def prepare_kernel(recv_count, plans, *refs):
+    offsets_hbm, channel_hbm, record_hbm, white_ref, choice_ref = refs[:5]
+    send_refs = refs[5 : 5 + len(plans)]
+    offsets_ref, channel_ref, record_ref, chosen_ref, sems = refs[5 + len(plans) :]
+    copies = [
+        pltpu.make_async_copy(offsets_hbm, offsets_ref, sems.at[0]),
+        pltpu.make_async_copy(channel_hbm, channel_ref, sems.at[1]),
+        pltpu.make_async_copy(record_hbm, record_ref, sems.at[2]),
+    ]
+    for copy in copies:
+        copy.start()
+    copies[1].wait()
     chan_dev = record_ref.shape[0]
+    owner = jnp.broadcast_to(channel_ref[...] // chan_dev, (recv_count, channel_ref.shape[1]))
+    held = jnp.sum(jnp.where(owner == iota(owner.shape, 0), 1, 0), axis=1, keepdims=True)
+    most = jnp.max(held)
+    chosen_ref[0] = sum((most > plan[0]).astype(jnp.int32) for plan in PLANS[:-1])
+    choosing = pltpu.make_async_copy(chosen_ref, choice_ref, sems.at[3])
+    choosing.start()
+    copies[0].wait()
+    copies[2].wait()
     start = offsets_ref[lax.axis_index("src")]
     first = start // LANES
     rest = start - first * LANES
@@ -66,6 +85,14 @@
     spread = jnp.broadcast_to(jnp.sqrt(power + EPSILON), (chan_dev, LANES))
     for tile in range(TILES):
         white_ref[:, tile * LANES : (tile + 1) * LANES] = (segment[tile] / spread).astype(jnp.bfloat16)
+    for plan, send_ref in zip(plans, send_refs, strict=True):
+        pack(plan, channel_ref, white_ref, send_ref)
+    choosing.wait()
+
+
+def pack(plan, channel_ref, white_ref, send_ref):
+    slots, split, rows = plan
+    chan_dev = white_ref.shape[0]
     base = lax.axis_index("recv") * chan_dev
     source = column(channel_ref[...])
     mine = iota((source.shape[0], chan_dev), 1) + base
@@ -140,9 +167,36 @@
         out_ref[:, n * LANES : (n + 1) * LANES] = part_ref[n].astype(jnp.bfloat16)
 
 
-def stack(plan, record, source_channel, band_edges, offsets):
-    slots, split, rows = plan
+def prepare(plans, record, source_channel, offsets):
     chan_dev = record.shape[0]
+    recv_count = lax.axis_size("recv")
+    channel_row = source_channel.reshape(1, source_channel.shape[0])
+    return pl.pallas_call(
+        functools.partial(prepare_kernel, recv_count, plans),
+        out_shape=[
+            jax.ShapeDtypeStruct((chan_dev, SEG), jnp.bfloat16),
+            jax.ShapeDtypeStruct((1,), jnp.int32),
+        ]
+        + [
+            jax.ShapeDtypeStruct((recv_count // CORES, rows, WL // split), jnp.bfloat16) for _, split, rows in plans
+        ],
+        in_specs=[pl.BlockSpec(memory_space=pl.ANY)] * 3,
+        out_specs=[VMEM, pl.BlockSpec(memory_space=pl.ANY)] + [VMEM] * len(plans),
+        scratch_shapes=[
+            pltpu.SMEM(offsets.shape, jnp.int32),
+            pltpu.VMEM(channel_row.shape, jnp.int32),
+            pltpu.VMEM(record.shape, record.dtype),
+            pltpu.SMEM((1,), jnp.int32),
+            pltpu.SemaphoreType.DMA((4,)),
+        ],
+        compiler_params=PARAMS,
+        name="prepare",
+    )(offsets, channel_row, record)
+
+
+def stack(number, record, source_channel, band_edges, offsets, white, *sends):
+    plan = PLANS[number]
+    chan_dev = white.shape[0]
     recv_index = lax.axis_index("recv")
     src_index = lax.axis_index("src")
     recv_count = lax.axis_size("recv")
@@ -151,17 +205,10 @@
     per = source_total // src_count
     wide = STEP * chan_dev
     channel_row = source_channel.reshape(1, source_total)
-    white, send = pl.pallas_call(
-        functools.partial(prepare_kernel, plan),
-        out_shape=(
-            jax.ShapeDtypeStruct((chan_dev, SEG), jnp.bfloat16),
-            jax.ShapeDtypeStruct((recv_count // CORES, rows, WL // split), jnp.bfloat16),
-        ),
-        in_specs=[SMEM, VMEM, VMEM],
-        out_specs=(VMEM, VMEM),
-        compiler_params=PARAMS,
-        name="prepare",
-    )(offsets, channel_row, record)
+    if number < EARLY:
+        send = sends[number]
+    else:
+        white, _, send = prepare([plan], record, source_channel, offsets)
     near = lax.all_to_all(
         send,
         "recv",
@@ -209,17 +256,16 @@
 
 
 def local(record, source_channel, band_edges, offsets):
-    blocks = jnp.arange(lax.axis_size("recv"), dtype=jnp.int32)
-    owners = source_channel // record.shape[0]
-    held = jnp.sum((owners[None, :] == blocks[:, None]).astype(jnp.int32), axis=1)
-    choice = jnp.max(sum((held > plan[0]).astype(jnp.int32) for plan in PLANS[:-1]))
+    white, choice, *sends = prepare(PLANS[:EARLY], record, source_channel, offsets)
     return lax.switch(
-        choice,
-        [functools.partial(stack, plan) for plan in PLANS],
+        choice[0],
+        [functools.partial(stack, number) for number in range(len(PLANS))],
         record,
         source_channel,
         band_edges,
         offsets,
+        white,
+        *sends,
     )
 
 

time: 59.2 us -> 57.8 us (0.976)
  other arithmetic: 1.57 us -> 0.15 us
    select_n x1 -> x0, other arithmetic: 0.66 us -> none  [local(): owners = source_channel // record.shape[0]]
    reduce_max x1 -> x0, other arithmetic: 0.64 us -> none  [local(): jnp.max(sum(((held > plan[0]).astype(jnp.int32) for plan in PLANS[:-1])))]
where the time goes in v5:
time: 57.8 us; the launch traced here: 57.6 us
  blocking collectives  47.2 us (82%)
  starting transfers between devices  4.05 us (7%)
  Pallas kernels  3.89 us (7%)
  local copies, waits for them, and re-layouts  0.99 us (2%)
  between operations  0.67 us (1%)
    all_to_all x1, blocking collectives, stack(): lax.all_to_all(partial, 'src', split_axis=0, concat_axis=0, tiled=True)  27.4 us
    all_to_all x1, blocking collectives, stack(): lax.all_to_all(send, 'recv', split_axis=0, concat_axis=0, tiled=True, axi...  19.9 us
    ppermute x1, starting transfers between devices, stack(): far = lax.ppermute(near, 'recv', [(i, i ^ 1) for i in range(recv_count)])  4.05 us
    pallas_call x1, Pallas kernels, stack(): pl.pallas_call(functools.partial(correlate_kernel, plan), out_shape=jax.S...  1.65 us
    pallas_call x1, Pallas kernels, prepare(): pl.pallas_call(functools.partial(prepare_kernel, recv_count, plans), out_...  1.42 us
  transfers between devices with their start and end apart: 1, of which 1 were waited for; matrix products, arithmetic and copies ran while one was open for 0% of the time, Pallas kernels for 1%

profile of v5, /device:TPU:1, one launch (start us, length us, event | category | flops | bytes accessed | tf_op | source)
XLA Modules:
  0.0 57.6 jit_solution(5272695804379758967)
XLA Ops:
  0.0 1.4 %prepare.5 = (bf16[16,2816]{1,0:T(8,128)(2,1)S(1)}, s32[1]{0:T(128)}, bf16[16,16,512]{2,1,0:T(8,128)(2,1)S(1)}, bf16[16,8,1280]{2,1,0:T(8,128)(2,1)S(1)}) custom-call(s32[16]{0:T(128)} %refs_0_.1, s32[1,32]{1,0:T(1,128)} %bitcast.46, bf16[16,8192]{1,0:T(8,128)(2,1)} %refs_2_.1), custom_call_target="tpu_custom_call" | custom-call | tf_op jit(solution)/shard_map/prepare/pallas_call | solution.py:174
  2.1 54.9 %conditional.1 = (f32[2,16,256]{2,1,0:T(8,128)S(1)}) conditional(s32[]{:T(128)} %bitcast.29, (s32[32]{0:T(128)}, bf16[16,16,512]{2,1,0:T(8,128)(2,1)S(1)}, s32[32,2]{0,1:T(2,128)}, bf16[16,2816]{1,0:T(8,128)(2,1)S(1)}) %tuple.25, (s32[32]{0:T(128)}, bf16[16,8,1280]{2,1,0:T(8,128)(2,1)S(1)}, s32[32,2]{0,1:T(2,128)}, ...), branch_computations={%region_0.2_spmd, %region_2.4_spmd, %region_4.6_spmd, %region_6.8_... | conditional | flops 1000270464 | bytes 12947722 | solution.py:260
  2.1 19.9 %all_to_all.32.near_ref = bf16[16,16,512]{2,1,0:T(8,128)(2,1)S(1)} all-to-all(bf16[16,16,512]{2,1,0:T(8,128)(2,1)S(1)} %get-tuple-element.42), channel_id=1, replica_groups={{0,32,64,96,128,160,192,224,256,288,320,352,384,416,448,480},{16,48,80,..., dimensions={0} | all-to-all | bytes 524288 | tf_op jit(solution)/shard_map/cond/branch_0_fun/all_to_all | solution.py:212
  22.0 4.0 %collective-permute-start = (bf16[16,16,512]{2,1,0:T(8,128)(2,1)S(1)}, bf16[16,16,512]{2,1,0:T(8,128)(2,1)S(1)}, u32[]{:S(2)}, u32[]{:S(2)}) collective-permute-start(bf16[16,16,512]{2,1,0:T(8,128)(2,1)S(1)} %all_to_all.32.near_ref), channel_id=1, source_target_pairs={{0,16},{16,0},{32,48},{48,32},{64,80},{80,64},{96,112},{112,96},{1... | collective-permute-start | bytes 786440 | tf_op jit(solution)/shard_map/cond/branch_0_fun/ppermute | solution.py:220
  26.0 0.0 copy-start.1
  26.0 0.0 copy-start.5
  26.1 0.8 %shift.4.shifted_ref = bf16[2816,256]{1,0:T(8,128)(2,1)S(1)} custom-call(bf16[16,2816]{1,0:T(8,128)(2,1)S(1)} %get-tuple-element.46.white_ref), custom_call_target="tpu_custom_call" | custom-call | flops 1000000000 | bytes 4000000 | tf_op jit(solution)/shard_map/cond/branch_0_fun/shift/pallas_call | solution.py:227
  26.9 0.3 collective-permute-done.far_ref
  27.2 0.0 copy-done.1
  27.2 0.1 dynamic_slice.17
  27.2 0.0 copy-done.5
  27.2 0.1 constant_dynamic-slice_fusion
  27.3 0.1 compare_and_fusion
  27.4 1.7 %correlate.4 = bf16[512,256]{1,0:T(8,128)(2,1)S(1)} custom-call(s32[1,32]{1,0:T(1,128)S(1)} %bitcast.47, bf16[16,16,512]{2,1,0:T(8,128)(2,1)S(1)} %all_to_all.32.near_ref, bf16[16,16,512]{2,1,0:T(8,128)(2,1)S(1)} %collective-permute-done.far_ref, bf16[2816,256]{1,0:T(8,128)(2,1)S(1)} %shift.4.shifted_ref), custom_call_target="tpu_custom_call" | custom-call | tf_op jit(solution)/shard_map/cond/branch_0_fun/correlate/pallas_call | solution.py:237
  29.1 27.4 %all_to_all.33 = bf16[16,32,256]{2,1,0:T(8,128)(2,1)S(1)} all-to-all(bf16[16,32,256]{2,1,0:T(8,128)(2,1)S(1)} %bitcast.42), channel_id=1, replica_groups=mesh['recv'=32,'src'=16] {'src'}, dimensions={0} | all-to-all | bytes 524288 | tf_op jit(solution)/shard_map/cond/branch_0_fun/all_to_all | solution.py:251
  56.5 0.1 mul.55
  56.6 0.1 copy.10
  57.0 0.0 copy-start
  57.0 0.6 %copy-done = f32[2,16,256]{2,1,0:T(8,128)} copy-done((f32[2,16,256]{2,1,0:T(8,128)}, f32[2,16,256]{2,1,0:T(8,128)S(1)}, u32[]{:S(2)}) %copy-start) | copy-done | bytes 32792
  (5 shorter events, 0.1 us)
Async XLA Ops:
  22.0 5.2 %collective-permute-start = (bf16[16,16,512]{2,1,0:T(8,128)(2,1)S(1)}, bf16[16,16,512]{2,1,0:T(8,128)(2,1)S(1)}, u32[]{:S(2)}, u32[]{:S(2)}) collective-permute-start(bf16[16,16,512]{2,1,0:T(8,128)(2,1)S(1)} %all_to_all.32.near_ref), channel_id=1, source_target_pairs={{0,16},{16,0},{32,48},{48,32},{64,80},{80,64},{96,112},{112,96},{1... | collective-permute-start | bytes 786440 | tf_op jit(solution)/shard_map/cond/branch_0_fun/ppermute | solution.py:220
  26.0 1.1 %copy-start.1 = (s32[32]{0:T(128)S(1)}, s32[32]{0:T(128)}, u32[]{:S(2)}) copy-start(s32[32]{0:T(128)} %get-tuple-element.48) | copy-start | bytes 388 | tf_op jit(solution)/shard_map/cond
  26.0 1.2 %copy-start.5 = (s32[32,2]{0,1:T(2,128)S(1)}, s32[32,2]{0,1:T(2,128)}, u32[]{:S(2)}) copy-start(s32[32,2]{0,1:T(2,128)} %get-tuple-element.47) | copy-start | bytes 772 | tf_op jit(solution)/shard_map/cond
  57.0 0.6 %copy-start = (f32[2,16,256]{2,1,0:T(8,128)}, f32[2,16,256]{2,1,0:T(8,128)S(1)}, u32[]{:S(2)}) copy-start(f32[2,16,256]{2,1,0:T(8,128)S(1)} %get-tuple-element.112) | copy-start | bytes 98308

commit v6 on v5

--- a/solution.py
+++ b/solution.py
@@ -18,6 +18,7 @@
 DEPTH = WL + LANES
 EPSILON = 1e-06
 CORES = 2
+PARTNERS = 2
 PLANS = ((3, 5, 16), (4, 2, 8), (6, 4, 24), (16, 1, 16))
 
 VMEM = pl.BlockSpec(memory_space=pltpu.VMEM)
@@ -124,17 +125,20 @@
         shifted_ref[at, :] = rows_ref[:, at].T
 
 
-def correlate_kernel(plan, channel_ref, near_ref, far_ref, shifted_ref, out_ref, a_ref, part_ref):
+def correlate_kernel(plan, flip, channel_ref, near_ref, far_ref, shifted_ref, out_ref, a_ref, part_ref):
     slots, split, rows = plan
     wide = shifted_ref.shape[1]
     chan_dev = wide // STEP
-    count = channel_ref.shape[1]
+    total_sources = channel_ref.shape[1]
+    count = total_sources // PARTNERS
     half = count // 2
     core = lax.rem(lax.axis_index("recv"), CORES)
-    order = iota((count, count), 0)
-    order = jnp.where(order < half, 2 * order, 2 * (order - half) + 1)
-    every = jnp.broadcast_to(channel_ref[...], (count, count))
-    source = jnp.sum(jnp.where(order == iota((count, count), 1), every, 0), axis=1, keepdims=True)
+    side = lax.rem(lax.axis_index("src") + flip, PARTNERS)
+    order = iota((count, total_sources), 0)
+    second = jnp.where(order < half, 0, 1)
+    order = 2 * (PARTNERS * (order - half * second) + side) + second
+    every = jnp.broadcast_to(channel_ref[...], (count, total_sources))
+    source = jnp.sum(jnp.where(order == iota((count, total_sources), 1), every, 0), axis=1, keepdims=True)
     owner = source // chan_dev
     place = jnp.sum(jnp.where((every >= owner * chan_dev) & (every < source), 1, 0), axis=1, keepdims=True)
     at = (owner // CORES) * rows + place
@@ -164,7 +168,7 @@
                         row : row + half, n * LANES : (n + 1) * LANES
                     ]
     for n in range(wide // LANES):
-        out_ref[:, n * LANES : (n + 1) * LANES] = part_ref[n].astype(jnp.bfloat16)
+        out_ref[:, n * LANES : (n + 1) * LANES] = part_ref[n].astype(out_ref.dtype)
 
 
 def prepare(plans, record, source_channel, offsets):
@@ -218,12 +222,6 @@
         axis_index_groups=[list(range(core, recv_count, CORES)) for core in range(CORES)],
     )
     far = lax.ppermute(near, "recv", [(i, i ^ 1) for i in range(recv_count)])
-    far, source_channel, band_edges = lax.optimization_barrier((far, source_channel, band_edges))
-    own_channel = lax.dynamic_slice_in_dim(source_channel, src_index * per, per, 0)
-    own_edges = lax.dynamic_slice_in_dim(band_edges, src_index * per, per, 0)
-    channel_ids = recv_index * chan_dev + jnp.arange(chan_dev, dtype=jnp.int32)
-    keep = (channel_ids[None, :] >= own_edges[:, 0:1]) & (channel_ids[None, :] < own_edges[:, 1:2])
-    keep = keep & (channel_ids[None, :] != own_channel[:, None])
     shifted = pl.pallas_call(
         shift_kernel,
         out_shape=jax.ShapeDtypeStruct((SEG, wide), jnp.bfloat16),
@@ -234,21 +232,43 @@
         cost_estimate=pl.CostEstimate(flops=10**9, bytes_accessed=4 * 10**6, transcendentals=0),
         name="shift",
     )(white)
-    partial = pl.pallas_call(
-        functools.partial(correlate_kernel, plan),
-        out_shape=jax.ShapeDtypeStruct((source_total * (L // STEP), wide), jnp.bfloat16),
-        in_specs=[VMEM, VMEM, VMEM, VMEM],
-        out_specs=VMEM,
-        scratch_shapes=[
-            pltpu.VMEM((source_total * COARSE, DEPTH), jnp.bfloat16),
-            pltpu.VMEM((wide // LANES, source_total * (L // STEP), LANES), jnp.float32),
-        ],
-        compiler_params=PARAMS,
-        name="correlate",
-    )(channel_row, near, far, shifted)
-    partial, keep = lax.optimization_barrier((partial, keep))
-    partial = partial.reshape(src_count, per * (L // STEP), wide)
-    windows = lax.all_to_all(partial, "src", split_axis=0, concat_axis=0, tiled=True)
+    deep = per * (L // STEP)
+    results = source_total // PARTNERS * (L // STEP)
+
+    def correlate(flip, dtype, name):
+        return pl.pallas_call(
+            functools.partial(correlate_kernel, plan, flip),
+            out_shape=jax.ShapeDtypeStruct((results, wide), dtype),
+            in_specs=[VMEM, VMEM, VMEM, VMEM],
+            out_specs=VMEM,
+            scratch_shapes=[
+                pltpu.VMEM((source_total // PARTNERS * COARSE, DEPTH), jnp.bfloat16),
+                pltpu.VMEM((wide // LANES, results, LANES), jnp.float32),
+            ],
+            compiler_params=PARAMS,
+            cost_estimate=pl.CostEstimate(flops=10**9, bytes_accessed=4 * 10**6, transcendentals=0),
+            name=name,
+        )(channel_row, near, far, shifted)
+
+    away = correlate(1, jnp.bfloat16, "away")
+    away, near, source_channel, band_edges = lax.optimization_barrier((away, near, source_channel, band_edges))
+    came = lax.ppermute(away, "src", [(i, i ^ 1) for i in range(src_count)])
+    home = correlate(0, jnp.float32, "home")
+    own_channel = lax.dynamic_slice_in_dim(source_channel, src_index * per, per, 0)
+    own_edges = lax.dynamic_slice_in_dim(band_edges, src_index * per, per, 0)
+    channel_ids = recv_index * chan_dev + jnp.arange(chan_dev, dtype=jnp.int32)
+    keep = (channel_ids[None, :] >= own_edges[:, 0:1]) & (channel_ids[None, :] < own_edges[:, 1:2])
+    keep = keep & (channel_ids[None, :] != own_channel[:, None])
+    home, keep = lax.optimization_barrier((home, keep))
+    partial = (home + came.astype(jnp.float32)).astype(jnp.bfloat16)
+    windows = lax.all_to_all(
+        partial.reshape(src_count // PARTNERS, deep, wide),
+        "src",
+        split_axis=0,
+        concat_axis=0,
+        tiled=True,
+        axis_index_groups=[list(range(side, src_count, PARTNERS)) for side in range(PARTNERS)],
+    )
     stacked = jnp.sum(windows.astype(jnp.float32), axis=0)
     stacked = stacked.reshape(per, L // STEP, STEP, chan_dev).transpose(0, 3, 1, 2).reshape(per, chan_dev, L)
     factor = 1.0 / float(WL * src_count) ** 0.5

time: 57.8 us -> 57.7 us (level)
  the two profiles are of different devices: /device:TPU:1 before, /device:TPU:64 now
where the time goes in v6:
time: 57.7 us; the launch traced here: 57 us
  blocking collectives  34.5 us (60%)
  starting transfers between devices  10.1 us (18%)
  waiting for transfers between devices  5.83 us (10%)
  Pallas kernels  4.42 us (8%)
  local copies, waits for them, and re-layouts  0.99 us (2%)
  between operations  0.67 us (1%)
    all_to_all x1, blocking collectives, stack(): lax.all_to_all(send, 'recv', split_axis=0, concat_axis=0, tiled=True, axi...  18.4 us
    all_to_all x1, blocking collectives, stack(): lax.all_to_all(partial.reshape(src_count // PARTNERS, deep, wide), 'src',...  16.1 us
    ppermute x1, starting transfers between devices, stack(): came = lax.ppermute(away, 'src', [(i, i ^ 1) for i in range(src_count)])  8.21 us
    ppermute x1, waiting for transfers between devices, stack(): came = lax.ppermute(away, 'src', [(i, i ^ 1) for i in range(src_count)])  5.18 us
    pallas_call x2, Pallas kernels, correlate(): pl.pallas_call(functools.partial(correlate_kernel, plan, flip), out_shape...  2.18 us
    ppermute x1, starting transfers between devices, stack(): far = lax.ppermute(near, 'recv', [(i, i ^ 1) for i in range(recv_count)])  1.91 us
    pallas_call x1, Pallas kernels, prepare(): pl.pallas_call(functools.partial(prepare_kernel, recv_count, plans), out_...  1.42 us
  transfers between devices with their start and end apart: 2, of which 2 were waited for; matrix products, arithmetic and copies ran while one was open for 0% of the time, Pallas kernels for 3%

profile of v6, /device:TPU:64, one launch (start us, length us, event | category | flops | bytes accessed | tf_op | source)
XLA Modules:
  0.0 57.0 jit_solution(17176058572345624975)
XLA Ops:
  0.0 1.4 %prepare.5 = (bf16[16,2816]{1,0:T(8,128)(2,1)S(1)}, s32[1]{0:T(128)}, bf16[16,16,512]{2,1,0:T(8,128)(2,1)S(1)}, bf16[16,8,1280]{2,1,0:T(8,128)(2,1)S(1)}) custom-call(s32[16]{0:T(128)} %refs_0_.1, s32[1,32]{1,0:T(1,128)} %bitcast.46, bf16[16,8192]{1,0:T(8,128)(2,1)} %refs_2_.1), custom_call_target="tpu_custom_call" | custom-call | tf_op jit(solution)/shard_map/prepare/pallas_call | solution.py:178
  2.1 54.3 %conditional.1 = (f32[2,16,256]{2,1,0:T(8,128)S(1)}) conditional(s32[]{:T(128)} %bitcast.29, (s32[32]{0:T(128)}, bf16[16,16,512]{2,1,0:T(8,128)(2,1)S(1)}, bf16[16,2816]{1,0:T(8,128)(2,1)S(1)}, s32[32,2]{0,1:T(2,128)}) %tuple.25, (s32[32]{0:T(128)}, bf16[16,8,1280]{2,1,0:T(8,128)(2,1)S(1)}, ...), branch_computations={%region_0.2_spmd, %region_2.4_spmd, %region_4.6_spmd, %region_6.8_... | conditional | flops 3000336128 | bytes 21603120 | solution.py:280
  2.1 18.4 %all_to_all.32.near_ref = bf16[16,16,512]{2,1,0:T(8,128)(2,1)S(1)} all-to-all(bf16[16,16,512]{2,1,0:T(8,128)(2,1)S(1)} %get-tuple-element.42), channel_id=1, replica_groups={{0,32,64,96,128,160,192,224,256,288,320,352,384,416,448,480},{16,48,80,..., dimensions={0} | all-to-all | bytes 524288 | tf_op jit(solution)/shard_map/cond/branch_0_fun/all_to_all | solution.py:216
  20.5 1.9 %collective-permute-start = (bf16[16,16,512]{2,1,0:T(8,128)(2,1)S(1)}, bf16[16,16,512]{2,1,0:T(8,128)(2,1)S(1)}, u32[]{:S(2)}, u32[]{:S(2)}) collective-permute-start(bf16[16,16,512]{2,1,0:T(8,128)(2,1)S(1)} %all_to_all.32.near_ref), channel_id=1, source_target_pairs={{0,16},{16,0},{32,48},{48,32},{64,80},{80,64},{96,112},{112,96},{1... | collective-permute-start | bytes 786440 | tf_op jit(solution)/shard_map/cond/branch_0_fun/ppermute | solution.py:224
  22.4 0.0 copy-start.5
  22.4 0.8 %shift.4.shifted_ref = bf16[2816,256]{1,0:T(8,128)(2,1)S(1)} custom-call(bf16[16,2816]{1,0:T(8,128)(2,1)S(1)} %get-tuple-element.44.white_ref), custom_call_target="tpu_custom_call" | custom-call | flops 1000000000 | bytes 4000000 | tf_op jit(solution)/shard_map/cond/branch_0_fun/shift/pallas_call | solution.py:225
  23.2 0.7 %collective-permute-done.far_ref = bf16[16,16,512]{2,1,0:T(8,128)(2,1)S(1)} collective-permute-done((bf16[16,16,512]{2,1,0:T(8,128)(2,1)S(1)}, bf16[16,16,512]{2,1,0:T(8,128)(2,1)S(1)}, u32[]{:S(2)}, u32[]{:S(2)}) %collective-permute-start) | collective-permute-done | bytes 262176 | tf_op jit(solution)/shard_map/cond/branch_0_fun/ppermute | solution.py:224
  23.9 0.0 copy-done.5
  23.9 0.0 copy-start.1
  23.9 1.1 %away.4 = bf16[256,256]{1,0:T(8,128)(2,1)S(1)} custom-call(s32[1,32]{1,0:T(1,128)S(1)} %bitcast.47, bf16[16,16,512]{2,1,0:T(8,128)(2,1)S(1)} %all_to_all.32.near_ref, bf16[16,16,512]{2,1,0:T(8,128)(2,1)S(1)} %collective-permute-done.far_ref, bf16[2816,256]{1,0:T(8,128)(2,1)S(1)} %shift.4.shifted_ref), custom_call_target="tpu_custom_call" | custom-call | flops 1000000000 | bytes 4000000 | tf_op jit(solution)/shard_map/cond/branch_0_fun/away/pallas_call | solution.py:239
  25.0 0.1 dynamic_slice.17
  25.1 0.0 copy-done.1
  25.1 0.1 constant_dynamic-slice_fusion
  25.1 8.2 %collective-permute-start.1 = (bf16[256,256]{1,0:T(8,128)(2,1)S(1)}, bf16[256,256]{1,0:T(8,128)(2,1)S(1)}, u32[]{:S(2)}, u32[]{:S(2)}) collective-permute-start(bf16[256,256]{1,0:T(8,128)(2,1)S(1)} %away.4), channel_id=1, source_target_pairs={{0,1},{1,0},{2,3},{3,2},{4,5},{5,4},{6,7},{7,6},{8,9},{9,8},{10,11... | collective-permute-start | bytes 393224 | tf_op jit(solution)/shard_map/cond/branch_0_fun/ppermute | solution.py:255
  33.4 0.1 compare_and_fusion
  33.4 1.1 %home.4 = f32[256,256]{1,0:T(8,128)S(1)} custom-call(s32[1,32]{1,0:T(1,128)S(1)} %bitcast.48, bf16[16,16,512]{2,1,0:T(8,128)(2,1)S(1)} %all_to_all.32.near_ref, bf16[16,16,512]{2,1,0:T(8,128)(2,1)S(1)} %collective-permute-done.far_ref, bf16[2816,256]{1,0:T(8,128)(2,1)S(1)} %shift.4.shifted_ref), custom_call_target="tpu_custom_call" | custom-call | flops 1000000000 | bytes 4000000 | tf_op jit(solution)/shard_map/cond/branch_0_fun/home/pallas_call | solution.py:239
  34.5 5.2 %collective-permute-done.1 = bf16[256,256]{1,0:T(8,128)(2,1)S(1)} collective-permute-done((bf16[256,256]{1,0:T(8,128)(2,1)S(1)}, bf16[256,256]{1,0:T(8,128)(2,1)S(1)}, u32[]{:S(2)}, u32[]{:S(2)}) %collective-permute-start.1) | collective-permute-done | bytes 131104 | tf_op jit(solution)/shard_map/cond/branch_0_fun/ppermute | solution.py:255
  39.7 16.1 %all_to_all.33 = bf16[8,32,256]{2,1,0:T(8,128)(2,1)S(1)} all-to-all(bf16[8,32,256]{2,1,0:T(8,128)(2,1)S(1)} %bitcast.42), channel_id=1, replica_groups={{0,2,4,6,8,10,12,14},{1,3,5,7,9,11,13,15},{16,18,20,22,24,26,28,30},{17..., dimensions={0} | all-to-all | bytes 262144 | tf_op jit(solution)/shard_map/cond/branch_0_fun/all_to_all | solution.py:264
  55.9 0.1 mul.55
  56.1 0.1 copy.10
  56.4 0.0 copy-start
  56.4 0.6 %copy-done = f32[2,16,256]{2,1,0:T(8,128)} copy-done((f32[2,16,256]{2,1,0:T(8,128)}, f32[2,16,256]{2,1,0:T(8,128)S(1)}, u32[]{:S(2)}) %copy-start) | copy-done | bytes 32792
  (6 shorter events, 0.1 us)
Async XLA Ops:
  20.5 3.4 %collective-permute-start = (bf16[16,16,512]{2,1,0:T(8,128)(2,1)S(1)}, bf16[16,16,512]{2,1,0:T(8,128)(2,1)S(1)}, u32[]{:S(2)}, u32[]{:S(2)}) collective-permute-start(bf16[16,16,512]{2,1,0:T(8,128)(2,1)S(1)} %all_to_all.32.near_ref), channel_id=1, source_target_pairs={{0,16},{16,0},{32,48},{48,32},{64,80},{80,64},{96,112},{112,96},{1... | collective-permute-start | bytes 786440 | tf_op jit(solution)/shard_map/cond/branch_0_fun/ppermute | solution.py:224
  22.4 1.5 %copy-start.5 = (s32[32]{0:T(128)S(1)}, s32[32]{0:T(128)}, u32[]{:S(2)}) copy-start(s32[32]{0:T(128)} %get-tuple-element.48) | copy-start | bytes 388 | tf_op jit(solution)/shard_map/cond
  23.9 1.2 %copy-start.1 = (s32[32,2]{0,1:T(2,128)S(1)}, s32[32,2]{0,1:T(2,128)}, u32[]{:S(2)}) copy-start(s32[32,2]{0,1:T(2,128)} %get-tuple-element.47) | copy-start | bytes 772 | tf_op jit(solution)/shard_map/cond
  25.1 14.6 %collective-permute-start.1 = (bf16[256,256]{1,0:T(8,128)(2,1)S(1)}, bf16[256,256]{1,0:T(8,128)(2,1)S(1)}, u32[]{:S(2)}, u32[]{:S(2)}) collective-permute-start(bf16[256,256]{1,0:T(8,128)(2,1)S(1)} %away.4), channel_id=1, source_target_pairs={{0,1},{1,0},{2,3},{3,2},{4,5},{5,4},{6,7},{7,6},{8,9},{9,8},{10,11... | collective-permute-start | bytes 393224 | tf_op jit(solution)/shard_map/cond/branch_0_fun/ppermute | solution.py:255
  56.4 0.6 %copy-start = (f32[2,16,256]{2,1,0:T(8,128)}, f32[2,16,256]{2,1,0:T(8,128)S(1)}, u32[]{:S(2)}) copy-start(f32[2,16,256]{2,1,0:T(8,128)S(1)} %get-tuple-element.124) | copy-start | bytes 98308

commit v7 on v6

--- a/solution.py
+++ b/solution.py
@@ -251,14 +251,17 @@
         )(channel_row, near, far, shifted)
 
     away = correlate(1, jnp.bfloat16, "away")
-    away, near, source_channel, band_edges = lax.optimization_barrier((away, near, source_channel, band_edges))
+    away, near, source_channel, band_edges, src_index = lax.optimization_barrier(
+        (away, near, source_channel, band_edges, src_index)
+    )
     came = lax.ppermute(away, "src", [(i, i ^ 1) for i in range(src_count)])
     home = correlate(0, jnp.float32, "home")
-    own_channel = lax.dynamic_slice_in_dim(source_channel, src_index * per, per, 0)
-    own_edges = lax.dynamic_slice_in_dim(band_edges, src_index * per, per, 0)
+    own = src_index * per + jnp.arange(per, dtype=jnp.int32)
+    own = own[:, None] == jnp.arange(source_total, dtype=jnp.int32)[None, :]
     channel_ids = recv_index * chan_dev + jnp.arange(chan_dev, dtype=jnp.int32)
-    keep = (channel_ids[None, :] >= own_edges[:, 0:1]) & (channel_ids[None, :] < own_edges[:, 1:2])
-    keep = keep & (channel_ids[None, :] != own_channel[:, None])
+    inside = (channel_ids[None, :] >= band_edges[:, 0:1]) & (channel_ids[None, :] < band_edges[:, 1:2])
+    inside = inside & (channel_ids[None, :] != source_channel[:, None])
+    keep = jnp.any(own[:, :, None] & inside[None, :, :], axis=1)
     home, keep = lax.optimization_barrier((home, keep))
     partial = (home + came.astype(jnp.float32)).astype(jnp.bfloat16)
     windows = lax.all_to_all(

time: 57.7 us -> 57.2 us (level)
  no operation moved by 1% of the time
where the time goes in v7:
time: 57.2 us; the launch traced here: 56.9 us
  blocking collectives  34.5 us (60%)
  starting transfers between devices  10.1 us (18%)
  waiting for transfers between devices  5.72 us (10%)
  Pallas kernels  4.42 us (8%)
  local copies, waits for them, and re-layouts  0.84 us (1%)
  between operations  0.67 us (1%)
    all_to_all x1, blocking collectives, stack(): lax.all_to_all(send, 'recv', split_axis=0, concat_axis=0, tiled=True, axi...  18.4 us
    all_to_all x1, blocking collectives, stack(): lax.all_to_all(partial.reshape(src_count // PARTNERS, deep, wide), 'src',...  16.1 us
    ppermute x1, starting transfers between devices, stack(): came = lax.ppermute(away, 'src', [(i, i ^ 1) for i in range(src_count)])  8.21 us
    ppermute x1, waiting for transfers between devices, stack(): came = lax.ppermute(away, 'src', [(i, i ^ 1) for i in range(src_count)])  5.06 us
    pallas_call x2, Pallas kernels, correlate(): pl.pallas_call(functools.partial(correlate_kernel, plan, flip), out_shape...  2.18 us
    ppermute x1, starting transfers between devices, stack(): far = lax.ppermute(near, 'recv', [(i, i ^ 1) for i in range(recv_count)])  1.91 us
    pallas_call x1, Pallas kernels, prepare(): pl.pallas_call(functools.partial(prepare_kernel, recv_count, plans), out_...  1.42 us
  transfers between devices with their start and end apart: 2, of which 2 were waited for; matrix products, arithmetic and copies ran while one was open for 0% of the time, Pallas kernels for 3%

profile of v7, /device:TPU:64, one launch (start us, length us, event | category | flops | bytes accessed | tf_op | source)
XLA Modules:
  0.0 56.9 jit_solution(353730639248216429)
XLA Ops:
  0.0 1.4 %prepare.5 = (bf16[16,2816]{1,0:T(8,128)(2,1)S(1)}, s32[1]{0:T(128)}, bf16[16,16,512]{2,1,0:T(8,128)(2,1)S(1)}, bf16[16,8,1280]{2,1,0:T(8,128)(2,1)S(1)}) custom-call(s32[16]{0:T(128)} %refs_0_.1, s32[1,32]{1,0:T(1,128)} %bitcast.46, bf16[16,8192]{1,0:T(8,128)(2,1)} %refs_2_.1), custom_call_target="tpu_custom_call" | custom-call | tf_op jit(solution)/shard_map/prepare/pallas_call | solution.py:178
  2.1 54.2 %conditional.1 = (f32[2,16,256]{2,1,0:T(8,128)S(1)}) conditional(s32[]{:T(128)} %bitcast.29, (s32[32]{0:T(128)}, bf16[16,16,512]{2,1,0:T(8,128)(2,1)S(1)}, bf16[16,2816]{1,0:T(8,128)(2,1)S(1)}, s32[32,2]{0,1:T(2,128)}) %tuple.25, (s32[32]{0:T(128)}, bf16[16,8,1280]{2,1,0:T(8,128)(2,1)S(1)}, ...), branch_computations={%region_0.3_spmd, %region_3.6_spmd, %region_6.9_spmd, %region_9.12... | conditional | flops 3000340480 | bytes 21605044 | solution.py:283
  2.1 18.4 %all_to_all.32.near_ref = bf16[16,16,512]{2,1,0:T(8,128)(2,1)S(1)} all-to-all(bf16[16,16,512]{2,1,0:T(8,128)(2,1)S(1)} %get-tuple-element.42), channel_id=1, replica_groups={{0,32,64,96,128,160,192,224,256,288,320,352,384,416,448,480},{16,48,80,..., dimensions={0} | all-to-all | bytes 524288 | tf_op jit(solution)/shard_map/cond/branch_0_fun/all_to_all | solution.py:216
  20.5 1.9 %collective-permute-start = (bf16[16,16,512]{2,1,0:T(8,128)(2,1)S(1)}, bf16[16,16,512]{2,1,0:T(8,128)(2,1)S(1)}, u32[]{:S(2)}, u32[]{:S(2)}) collective-permute-start(bf16[16,16,512]{2,1,0:T(8,128)(2,1)S(1)} %all_to_all.32.near_ref), channel_id=1, source_target_pairs={{0,16},{16,0},{32,48},{48,32},{64,80},{80,64},{96,112},{112,96},{1... | collective-permute-start | bytes 786440 | tf_op jit(solution)/shard_map/cond/branch_0_fun/ppermute | solution.py:224
  22.4 0.0 copy-start
  22.4 0.8 %shift.4.shifted_ref = bf16[2816,256]{1,0:T(8,128)(2,1)S(1)} custom-call(bf16[16,2816]{1,0:T(8,128)(2,1)S(1)} %get-tuple-element.44.white_ref), custom_call_target="tpu_custom_call" | custom-call | flops 1000000000 | bytes 4000000 | tf_op jit(solution)/shard_map/cond/branch_0_fun/shift/pallas_call | solution.py:225
  23.2 0.7 %collective-permute-done.far_ref = bf16[16,16,512]{2,1,0:T(8,128)(2,1)S(1)} collective-permute-done((bf16[16,16,512]{2,1,0:T(8,128)(2,1)S(1)}, bf16[16,16,512]{2,1,0:T(8,128)(2,1)S(1)}, u32[]{:S(2)}, u32[]{:S(2)}) %collective-permute-start) | collective-permute-done | bytes 262176 | tf_op jit(solution)/shard_map/cond/branch_0_fun/ppermute | solution.py:224
  23.9 0.0 copy-done
  23.9 0.0 copy-start.5
  23.9 1.1 %away.4 = bf16[256,256]{1,0:T(8,128)(2,1)S(1)} custom-call(s32[1,32]{1,0:T(1,128)S(1)} %bitcast.47, bf16[16,16,512]{2,1,0:T(8,128)(2,1)S(1)} %all_to_all.32.near_ref, bf16[16,16,512]{2,1,0:T(8,128)(2,1)S(1)} %collective-permute-done.far_ref, bf16[2816,256]{1,0:T(8,128)(2,1)S(1)} %shift.4.shifted_ref), custom_call_target="tpu_custom_call" | custom-call | flops 1000000000 | bytes 4000000 | tf_op jit(solution)/shard_map/cond/branch_0_fun/away/pallas_call | solution.py:239
  25.0 0.0 copy-done.5
  25.0 0.1 iota_compare_fusion
  25.1 8.2 %collective-permute-start.1 = (bf16[256,256]{1,0:T(8,128)(2,1)S(1)}, bf16[256,256]{1,0:T(8,128)(2,1)S(1)}, u32[]{:S(2)}, u32[]{:S(2)}) collective-permute-start(bf16[256,256]{1,0:T(8,128)(2,1)S(1)} %away.4), channel_id=1, source_target_pairs={{0,1},{1,0},{2,3},{3,2},{4,5},{5,4},{6,7},{7,6},{8,9},{9,8},{10,11... | collective-permute-start | bytes 393224 | tf_op jit(solution)/shard_map/cond/branch_0_fun/ppermute | solution.py:257
  33.3 0.1 compare_and_fusion
  33.4 1.1 %home.4 = f32[256,256]{1,0:T(8,128)S(1)} custom-call(s32[1,32]{1,0:T(1,128)S(1)} %bitcast.48, bf16[16,16,512]{2,1,0:T(8,128)(2,1)S(1)} %all_to_all.32.near_ref, bf16[16,16,512]{2,1,0:T(8,128)(2,1)S(1)} %collective-permute-done.far_ref, bf16[2816,256]{1,0:T(8,128)(2,1)S(1)} %shift.4.shifted_ref), custom_call_target="tpu_custom_call" | custom-call | flops 1000000000 | bytes 4000000 | tf_op jit(solution)/shard_map/cond/branch_0_fun/home/pallas_call | solution.py:239
  34.5 0.1 and_reduce_fusion
  34.6 5.1 %collective-permute-done.1 = bf16[256,256]{1,0:T(8,128)(2,1)S(1)} collective-permute-done((bf16[256,256]{1,0:T(8,128)(2,1)S(1)}, bf16[256,256]{1,0:T(8,128)(2,1)S(1)}, u32[]{:S(2)}, u32[]{:S(2)}) %collective-permute-start.1) | collective-permute-done | bytes 131104 | tf_op jit(solution)/shard_map/cond/branch_0_fun/ppermute | solution.py:257
  39.7 16.1 %all_to_all.33 = bf16[8,32,256]{2,1,0:T(8,128)(2,1)S(1)} all-to-all(bf16[8,32,256]{2,1,0:T(8,128)(2,1)S(1)} %bitcast.42), channel_id=1, replica_groups={{0,2,4,6,8,10,12,14},{1,3,5,7,9,11,13,15},{16,18,20,22,24,26,28,30},{17..., dimensions={0} | all-to-all | bytes 262144 | tf_op jit(solution)/shard_map/cond/branch_0_fun/all_to_all | solution.py:267
  55.8 0.1 mul.51
  56.0 0.1 copy.11
  56.3 0.0 copy-start.4
  56.3 0.6 %copy-done.4 = f32[2,16,256]{2,1,0:T(8,128)} copy-done((f32[2,16,256]{2,1,0:T(8,128)}, f32[2,16,256]{2,1,0:T(8,128)S(1)}, u32[]{:S(2)}) %copy-start.4) | copy-done | bytes 32792
  (7 shorter events, 0.1 us)
Async XLA Ops:
  20.5 3.4 %collective-permute-start = (bf16[16,16,512]{2,1,0:T(8,128)(2,1)S(1)}, bf16[16,16,512]{2,1,0:T(8,128)(2,1)S(1)}, u32[]{:S(2)}, u32[]{:S(2)}) collective-permute-start(bf16[16,16,512]{2,1,0:T(8,128)(2,1)S(1)} %all_to_all.32.near_ref), channel_id=1, source_target_pairs={{0,16},{16,0},{32,48},{48,32},{64,80},{80,64},{96,112},{112,96},{1... | collective-permute-start | bytes 786440 | tf_op jit(solution)/shard_map/cond/branch_0_fun/ppermute | solution.py:224
  22.4 1.5 %copy-start = (s32[32]{0:T(128)S(1)}, s32[32]{0:T(128)}, u32[]{:S(2)}) copy-start(s32[32]{0:T(128)} %get-tuple-element.49) | copy-start | bytes 388 | tf_op jit(solution)/shard_map/cond
  23.9 1.1 %copy-start.5 = (s32[32,2]{0,1:T(2,128)S(1)}, s32[32,2]{0,1:T(2,128)}, u32[]{:S(2)}) copy-start(s32[32,2]{0,1:T(2,128)} %get-tuple-element.48) | copy-start | bytes 772 | tf_op jit(solution)/shard_map/cond
  25.1 14.6 %collective-permute-start.1 = (bf16[256,256]{1,0:T(8,128)(2,1)S(1)}, bf16[256,256]{1,0:T(8,128)(2,1)S(1)}, u32[]{:S(2)}, u32[]{:S(2)}) collective-permute-start(bf16[256,256]{1,0:T(8,128)(2,1)S(1)} %away.4), channel_id=1, source_target_pairs={{0,1},{1,0},{2,3},{3,2},{4,5},{5,4},{6,7},{7,6},{8,9},{9,8},{10,11... | collective-permute-start | bytes 393224 | tf_op jit(solution)/shard_map/cond/branch_0_fun/ppermute | solution.py:257
  56.3 0.6 %copy-start.4 = (f32[2,16,256]{2,1,0:T(8,128)}, f32[2,16,256]{2,1,0:T(8,128)S(1)}, u32[]{:S(2)}) copy-start(f32[2,16,256]{2,1,0:T(8,128)S(1)} %get-tuple-element.127) | copy-start | bytes 98308
